TPU v7x, 32 devices: a whole 2x2x4 slice. The times are simulated.
32 devices in a mesh: dp: 2 (over y), fsdp: 16 (over z, x, core).
Axes of the slice: x: 2, y: 2, z: 4, core: 2. Of those that a mesh axis runs over, the one named last changes fastest.
Arguments:
- block_input: bfloat16 [64, 512, 768], P(('dp', 'fsdp')), may hold values from -6 to 6
- segment_ids: int32 [64, 512], P(('dp', 'fsdp')), may hold values from 0 to 7, never falling along the last dimension, each value on 1 to 192 neighbouring positions
- cotangent: bfloat16 [64, 512, 768], P(('dp', 'fsdp')), may hold values from -12 to 12
- w_query: bfloat16 [768, 768], P(('dp', 'fsdp')), may hold values from -0.3125 to 0.3125
- b_query: bfloat16 [768], P(('dp', 'fsdp')), may hold values from -3 to 3
- w_key: bfloat16 [768, 768], P(('dp', 'fsdp')), may hold values from -0.3125 to 0.3125
- w_value: bfloat16 [768, 768], P(('dp', 'fsdp')), may hold values from -0.21875 to 0.21875
- b_value: bfloat16 [768], P(('dp', 'fsdp')), may hold values from -3 to 3
- w_out: bfloat16 [768, 768], P(('dp', 'fsdp')), may hold values from -1.25 to 1.25
- b_out: bfloat16 [768], P(('dp', 'fsdp')), may hold values from -3 to 3
- gain_one: bfloat16 [768], P(('dp', 'fsdp')), may hold values from 0.25 to 1.75
- shift_one: bfloat16 [768], P(('dp', 'fsdp')), may hold values from -3 to 3
- w_inner: bfloat16 [768, 3072], P(('dp', 'fsdp')), may hold values from -0.21875 to 0.21875
- b_inner: bfloat16 [3072], P(('dp', 'fsdp')), may hold values from -3 to 3
- w_outer: bfloat16 [3072, 768], P(('dp', 'fsdp')), may hold values from -0.15625 to 0.15625
- b_outer: bfloat16 [768], P(('dp', 'fsdp')), may hold values from -3 to 3
- gain_two: bfloat16 [768], P(('dp', 'fsdp')), may hold values from 0.25 to 1.75
- shift_two: bfloat16 [768], P(('dp', 'fsdp')), may hold values from -3 to 3
Outputs:
- layer_out: bfloat16 [64, 512, 768], P(('dp', 'fsdp'))
- grad_input: bfloat16 [64, 512, 768], P(('dp', 'fsdp'))
- grad_w_query: float32 [768, 768], P(('dp', 'fsdp'))
- grad_b_query: float32 [768], P(('dp', 'fsdp'))
- grad_w_key: float32 [768, 768], P(('dp', 'fsdp'))
- grad_w_value: float32 [768, 768], P(('dp', 'fsdp'))
- grad_b_value: float32 [768], P(('dp', 'fsdp'))
- grad_w_out: float32 [768, 768], P(('dp', 'fsdp'))
- grad_b_out: float32 [768], P(('dp', 'fsdp'))
- grad_gain_one: float32 [768], P(('dp', 'fsdp'))
- grad_shift_one: float32 [768], P(('dp', 'fsdp'))
- grad_w_inner: float32 [768, 3072], P(('dp', 'fsdp'))
- grad_b_inner: float32 [3072], P(('dp', 'fsdp'))
- grad_w_outer: float32 [3072, 768], P(('dp', 'fsdp'))
- grad_b_outer: float32 [768], P(('dp', 'fsdp'))
- grad_gain_two: float32 [768], P(('dp', 'fsdp'))
- grad_shift_two: float32 [768], P(('dp', 'fsdp'))
Inputs may be any that keep to these rules, and one draw needn't show every extreme that they name: `segment_ids`: along each row the numbers never fall; one document has 1 to 192 tokens, and some document has exactly 192.
All inputs are finite; a program needn't handle non-finite values.
Results may differ from a plain program's by a relative error of at most 0.015.
The roundings to bfloat16 on the way count: a program that leaves them out, or rounds other values in their place, can miss the bound.
Values may be sent and summed in bfloat16 or wider, within the bound.
No kernel may reach another device: no remote copies, remote signals or barrier semaphores. Data moves between devices by JAX's collectives and lax.ppermute only.
A program may use at most 192 MiB of HBM per device.

v0:
```python
from functools import partial

import jax
import jax.numpy as jnp
from jax import lax
from jax.sharding import PartitionSpec as P

D = 768
HEADS = 12
HEAD_DIM = 64
SEQ = 512


epsilon_norm = 1e-05


def layer_norm(hidden, gain_vec, shift_vec):
    mean_val = jnp.mean(hidden, axis=-1, keepdims=True)
    centred = hidden - mean_val
    variance = jnp.mean(centred * centred, axis=-1, keepdims=True)
    return centred * lax.rsqrt(variance + epsilon_norm) * gain_vec + shift_vec


def matmul(left, right):
    return jnp.dot(left, right, preferred_element_type=jnp.float32)


def to_float(vector):
    return vector.astype(jnp.float32)


def soft_probs(query_heads, key_heads, same_segment, log_total):
    scores = jnp.einsum(
        "bqhd,bkhd->bhqk", query_heads, key_heads, preferred_element_type=jnp.float32
    ) * HEAD_DIM ** (-0.5)
    masked = jnp.where(same_segment[:, None], scores, -1e30)
    return (masked, jnp.exp(masked - log_total))


def forward(tokens, same_segment, params):
    (
        w_query,
        b_query,
        w_key,
        w_value,
        b_value,
        w_out,
        b_out,
        gain_one,
        shift_one,
        w_inner,
        b_inner,
        w_outer,
        b_outer,
        gain_two,
        shift_two,
    ) = params
    seq_count = tokens.shape[0]
    row_count = seq_count * SEQ
    flat_rows = tokens.reshape(row_count, D)
    queries = (matmul(flat_rows, w_query) + to_float(b_query)).astype(jnp.bfloat16)
    key_rows = matmul(flat_rows, w_key).astype(jnp.bfloat16)
    values = (matmul(flat_rows, w_value) + to_float(b_value)).astype(jnp.bfloat16)
    query_heads = queries.reshape(seq_count, SEQ, HEADS, HEAD_DIM)
    key_heads = key_rows.reshape(seq_count, SEQ, HEADS, HEAD_DIM)
    value_heads = values.reshape(seq_count, SEQ, HEADS, HEAD_DIM)
    scores = jnp.einsum(
        "bqhd,bkhd->bhqk", query_heads, key_heads, preferred_element_type=jnp.float32
    ) * HEAD_DIM ** (-0.5)
    masked = jnp.where(same_segment[:, None], scores, -1e30)
    row_max = jnp.max(masked, axis=-1, keepdims=True)
    total = jnp.sum(jnp.exp(masked - row_max), axis=-1, keepdims=True)
    log_total = row_max + jnp.log(total)
    probs_low = jnp.exp(masked - log_total).astype(jnp.bfloat16)
    context = jnp.einsum(
        "bhqk,bkhd->bqhd", probs_low, value_heads, preferred_element_type=jnp.float32
    )
    context = context.reshape(row_count, D).astype(jnp.bfloat16)
    attention = matmul(context, w_out) + to_float(b_out)
    hidden_one = flat_rows.astype(jnp.float32) + attention
    normed_one = layer_norm(hidden_one, to_float(gain_one), to_float(shift_one))
    normed_low = normed_one.astype(jnp.bfloat16)
    pre_act = matmul(normed_low, w_inner) + to_float(b_inner)
    activated = jax.nn.gelu(pre_act, approximate=True).astype(jnp.bfloat16)
    branch = matmul(activated, w_outer) + to_float(b_outer)
    hidden_two = normed_one + branch
    result = layer_norm(hidden_two, to_float(gain_two), to_float(shift_two)).astype(jnp.bfloat16)
    kept = (
        query_heads,
        key_heads,
        value_heads,
        log_total,
        context,
        hidden_one,
        normed_low,
        pre_act,
        activated,
        hidden_two,
    )
    return (result.reshape(tokens.shape), kept)


def backward_ffn(cotangent, params, kept):
    (
        w_query,
        b_query,
        w_key,
        w_value,
        b_value,
        w_out,
        b_out,
        gain_one,
        shift_one,
        w_inner,
        b_inner,
        w_outer,
        b_outer,
        gain_two,
        shift_two,
    ) = params
    (
        query_heads,
        key_heads,
        value_heads,
        log_total,
        context,
        hidden_one,
        normed_low,
        pre_act,
        activated,
        hidden_two,
    ) = kept
    grad_rows = cotangent.reshape(hidden_two.shape).astype(jnp.float32)
    unused_two, norm_back = jax.vjp(layer_norm, hidden_two, to_float(gain_two), to_float(shift_two))
    d_hidden_two, d_gain_two, d_shift_two = norm_back(grad_rows)
    d_branch = d_hidden_two.astype(jnp.bfloat16)
    d_b_outer = jnp.sum(d_branch.astype(jnp.float32), axis=0)
    d_w_outer = jnp.einsum("nf,nd->fd", activated, d_branch, preferred_element_type=jnp.float32)
    d_activated = jnp.einsum("nd,fd->nf", d_branch, w_outer, preferred_element_type=jnp.float32)
    unused_act, gelu_back = jax.vjp(partial(jax.nn.gelu, approximate=True), pre_act)
    d_pre = gelu_back(d_activated)[0].astype(jnp.bfloat16)
    d_b_inner = jnp.sum(d_pre.astype(jnp.float32), axis=0)
    d_w_inner = jnp.einsum("nd,nf->df", normed_low, d_pre, preferred_element_type=jnp.float32)
    d_normed = d_hidden_two + jnp.einsum(
        "nf,df->nd", d_pre, w_inner, preferred_element_type=jnp.float32
    )
    return (d_normed, (d_w_inner, d_b_inner, d_w_outer, d_b_outer, d_gain_two, d_shift_two))


def backward_attention(tokens, same_segment, d_normed, params, kept):
    (
        w_query,
        b_query,
        w_key,
        w_value,
        b_value,
        w_out,
        b_out,
        gain_one,
        shift_one,
        w_inner,
        b_inner,
        w_outer,
        b_outer,
        gain_two,
        shift_two,
    ) = params
    (
        query_heads,
        key_heads,
        value_heads,
        log_total,
        context,
        hidden_one,
        normed_low,
        pre_act,
        activated,
        hidden_two,
    ) = kept
    seq_count = tokens.shape[0]
    row_count = seq_count * SEQ
    flat_rows = tokens.reshape(row_count, D)
    unused_one, norm_back = jax.vjp(layer_norm, hidden_one, to_float(gain_one), to_float(shift_one))
    d_hidden_one, d_gain_one, d_shift_one = norm_back(d_normed)
    d_attention = d_hidden_one.astype(jnp.bfloat16)
    d_b_out = jnp.sum(d_attention.astype(jnp.float32), axis=0)
    d_w_out = jnp.einsum("nd,ne->de", context, d_attention, preferred_element_type=jnp.float32)
    d_context = jnp.einsum("ne,de->nd", d_attention, w_out, preferred_element_type=jnp.float32)
    d_context = d_context.astype(jnp.bfloat16).reshape(seq_count, SEQ, HEADS, HEAD_DIM)
    masked, probs = soft_probs(query_heads, key_heads, same_segment, log_total)
    d_probs = jnp.einsum(
        "bqhd,bkhd->bhqk", d_context, value_heads, preferred_element_type=jnp.float32
    )
    d_values = jnp.einsum(
        "bhqk,bqhd->bkhd", probs.astype(jnp.bfloat16), d_context, preferred_element_type=jnp.float32
    ).astype(jnp.bfloat16)
    d_scores = probs * (d_probs - jnp.sum(probs * d_probs, axis=-1, keepdims=True))
    d_scores = d_scores.astype(jnp.bfloat16)
    score_scale = HEAD_DIM ** (-0.5)
    d_queries = (
        jnp.einsum("bhqk,bkhd->bqhd", d_scores, key_heads, preferred_element_type=jnp.float32)
        * score_scale
    ).astype(jnp.bfloat16)
    d_keys = (
        jnp.einsum("bhqk,bqhd->bkhd", d_scores, query_heads, preferred_element_type=jnp.float32)
        * score_scale
    ).astype(jnp.bfloat16)
    d_queries = d_queries.reshape(row_count, D)
    d_keys = d_keys.reshape(row_count, D)
    d_values = d_values.reshape(row_count, D)
    d_w_query = jnp.einsum("nd,ne->de", flat_rows, d_queries, preferred_element_type=jnp.float32)
    d_w_key = jnp.einsum("nd,ne->de", flat_rows, d_keys, preferred_element_type=jnp.float32)
    d_w_value = jnp.einsum("nd,ne->de", flat_rows, d_values, preferred_element_type=jnp.float32)
    d_b_query = jnp.sum(d_queries.astype(jnp.float32), axis=0)
    d_b_value = jnp.sum(d_values.astype(jnp.float32), axis=0)
    d_input = (
        d_hidden_one
        + jnp.einsum("ne,de->nd", d_queries, w_query, preferred_element_type=jnp.float32)
        + jnp.einsum("ne,de->nd", d_keys, w_key, preferred_element_type=jnp.float32)
        + jnp.einsum("ne,de->nd", d_values, w_value, preferred_element_type=jnp.float32)
    )
    d_input = d_input.astype(jnp.bfloat16).reshape(tokens.shape)
    return (
        d_input,
        (
            d_w_query,
            d_b_query,
            d_w_key,
            d_w_value,
            d_b_value,
            d_w_out,
            d_b_out,
            d_gain_one,
            d_shift_one,
        ),
    )


def on_device(
    block_input,
    segment_ids,
    cotangent,
    w_query,
    b_query,
    w_key,
    w_value,
    b_value,
    w_out,
    b_out,
    gain_one,
    shift_one,
    w_inner,
    b_inner,
    w_outer,
    b_outer,
    gain_two,
    shift_two,
):
    same_segment = segment_ids[:, :, None] == segment_ids[:, None, :]
    params = (
        lax.all_gather(w_query, ("dp", "fsdp"), axis=0, tiled=True),
        lax.all_gather(b_query, ("dp", "fsdp"), axis=0, tiled=True),
        lax.all_gather(w_key, ("dp", "fsdp"), axis=0, tiled=True),
        lax.all_gather(w_value, ("dp", "fsdp"), axis=0, tiled=True),
        lax.all_gather(b_value, ("dp", "fsdp"), axis=0, tiled=True),
        lax.all_gather(w_out, ("dp", "fsdp"), axis=0, tiled=True),
        lax.all_gather(b_out, ("dp", "fsdp"), axis=0, tiled=True),
        lax.all_gather(gain_one, ("dp", "fsdp"), axis=0, tiled=True),
        lax.all_gather(shift_one, ("dp", "fsdp"), axis=0, tiled=True),
        lax.all_gather(w_inner, ("dp", "fsdp"), axis=0, tiled=True),
        lax.all_gather(b_inner, ("dp", "fsdp"), axis=0, tiled=True),
        lax.all_gather(w_outer, ("dp", "fsdp"), axis=0, tiled=True),
        lax.all_gather(b_outer, ("dp", "fsdp"), axis=0, tiled=True),
        lax.all_gather(gain_two, ("dp", "fsdp"), axis=0, tiled=True),
        lax.all_gather(shift_two, ("dp", "fsdp"), axis=0, tiled=True),
    )
    result, kept = forward(block_input, same_segment, params)
    params = (
        lax.all_gather(w_query, ("dp", "fsdp"), axis=0, tiled=True),
        lax.all_gather(b_query, ("dp", "fsdp"), axis=0, tiled=True),
        lax.all_gather(w_key, ("dp", "fsdp"), axis=0, tiled=True),
        lax.all_gather(w_value, ("dp", "fsdp"), axis=0, tiled=True),
        lax.all_gather(b_value, ("dp", "fsdp"), axis=0, tiled=True),
        lax.all_gather(w_out, ("dp", "fsdp"), axis=0, tiled=True),
        lax.all_gather(b_out, ("dp", "fsdp"), axis=0, tiled=True),
        lax.all_gather(gain_one, ("dp", "fsdp"), axis=0, tiled=True),
        lax.all_gather(shift_one, ("dp", "fsdp"), axis=0, tiled=True),
        lax.all_gather(w_inner, ("dp", "fsdp"), axis=0, tiled=True),
        lax.all_gather(b_inner, ("dp", "fsdp"), axis=0, tiled=True),
        lax.all_gather(w_outer, ("dp", "fsdp"), axis=0, tiled=True),
        lax.all_gather(b_outer, ("dp", "fsdp"), axis=0, tiled=True),
        lax.all_gather(gain_two, ("dp", "fsdp"), axis=0, tiled=True),
        lax.all_gather(shift_two, ("dp", "fsdp"), axis=0, tiled=True),
    )
    result_again, kept = forward(block_input, same_segment, params)
    d_normed, ffn_terms = backward_ffn(cotangent, params, kept)
    d_w_inner, d_b_inner, d_w_outer, d_b_outer, d_gain_two, d_shift_two = ffn_terms
    d_input, attention_terms = backward_attention(block_input, same_segment, d_normed, params, kept)
    (
        d_w_query,
        d_b_query,
        d_w_key,
        d_w_value,
        d_b_value,
        d_w_out,
        d_b_out,
        d_gain_one,
        d_shift_one,
    ) = attention_terms
    shards = (
        lax.psum_scatter(d_w_query, ("dp", "fsdp"), scatter_dimension=0, tiled=True),
        lax.psum_scatter(d_b_query, ("dp", "fsdp"), scatter_dimension=0, tiled=True),
        lax.psum_scatter(d_w_key, ("dp", "fsdp"), scatter_dimension=0, tiled=True),
        lax.psum_scatter(d_w_value, ("dp", "fsdp"), scatter_dimension=0, tiled=True),
        lax.psum_scatter(d_b_value, ("dp", "fsdp"), scatter_dimension=0, tiled=True),
        lax.psum_scatter(d_w_out, ("dp", "fsdp"), scatter_dimension=0, tiled=True),
        lax.psum_scatter(d_b_out, ("dp", "fsdp"), scatter_dimension=0, tiled=True),
        lax.psum_scatter(d_gain_one, ("dp", "fsdp"), scatter_dimension=0, tiled=True),
        lax.psum_scatter(d_shift_one, ("dp", "fsdp"), scatter_dimension=0, tiled=True),
        lax.psum_scatter(d_w_inner, ("dp", "fsdp"), scatter_dimension=0, tiled=True),
        lax.psum_scatter(d_b_inner, ("dp", "fsdp"), scatter_dimension=0, tiled=True),
        lax.psum_scatter(d_w_outer, ("dp", "fsdp"), scatter_dimension=0, tiled=True),
        lax.psum_scatter(d_b_outer, ("dp", "fsdp"), scatter_dimension=0, tiled=True),
        lax.psum_scatter(d_gain_two, ("dp", "fsdp"), scatter_dimension=0, tiled=True),
        lax.psum_scatter(d_shift_two, ("dp", "fsdp"), scatter_dimension=0, tiled=True),
    )
    return (
        result,
        d_input,
        shards[0],
        shards[1],
        shards[2],
        shards[3],
        shards[4],
        shards[5],
        shards[6],
        shards[7],
        shards[8],
        shards[9],
        shards[10],
        shards[11],
        shards[12],
        shards[13],
        shards[14],
    )


def solution(mesh):
    placed = (
        P(("dp", "fsdp"), None, None),
        P(("dp", "fsdp"), None),
        P(("dp", "fsdp"), None, None),
        P(("dp", "fsdp"), None),
        P(("dp", "fsdp")),
        P(("dp", "fsdp"), None),
        P(("dp", "fsdp"), None),
        P(("dp", "fsdp")),
        P(("dp", "fsdp"), None),
        P(("dp", "fsdp")),
        P(("dp", "fsdp")),
        P(("dp", "fsdp")),
        P(("dp", "fsdp"), None),
        P(("dp", "fsdp")),
        P(("dp", "fsdp"), None),
        P(("dp", "fsdp")),
        P(("dp", "fsdp")),
        P(("dp", "fsdp")),
    )
    return jax.shard_map(
        on_device,
        mesh=mesh,
        in_specs=placed,
        out_specs=(
            P(("dp", "fsdp"), None, None),
            P(("dp", "fsdp"), None, None),
            P(("dp", "fsdp"), None),
            P(("dp", "fsdp")),
            P(("dp", "fsdp"), None),
            P(("dp", "fsdp"), None),
            P(("dp", "fsdp")),
            P(("dp", "fsdp"), None),
            P(("dp", "fsdp")),
            P(("dp", "fsdp")),
            P(("dp", "fsdp")),
            P(("dp", "fsdp"), None),
            P(("dp", "fsdp")),
            P(("dp", "fsdp"), None),
            P(("dp", "fsdp")),
            P(("dp", "fsdp")),
            P(("dp", "fsdp")),
        ),
        check_vma=False,
    )
```

profile of v0, /device:TPU:0, one launch (start us, length us, event | category | flops | bytes accessed | tf_op | source)
XLA Modules:
  0.0 1126.5 jit_solution(3051037126555261307)
XLA Ops:
  18.8 42.4 %all-reduce.19 = (bf16[768]{0:T(1024)(128)(2,1)S(1)}, bf16[768]{0:T(1024)(128)(2,1)S(1)}, bf16[768]{0:T(1024)(128)(2,1)S(1)}, bf16[768]{0:T(1024)(128)(2,1)S(1)}...) all-reduce(bf16[768]{0:T(1024)(128)(2,1)S(1)} %dynamic-update-slice, ...), channel_id=1, replica_groups=mesh['dp'=2,'fsdp'=16] {'dp','fsdp'}, use_global_device_ids=true, to_apply=%add | all-reduce | flops 9216 | bytes 36864
  73.0 50.9 %all-gather.7.cloned.1.call-done = bf16[768,768]{1,0:T(8,128)(2,1)} async-done(((bf16[24,768]{1,0:T(8,128)(2,1)}), bf16[768,768]{1,0:T(8,128)(2,1)}) %all-gather.7.cloned.1.call-update) | async-done | bytes 1179664 | tf_op jit(solution)/shard_map/all_gather | solution.py:264
  132.2 47.5 %all-gather.11.cloned.1.call-done = bf16[768,768]{1,0:T(8,128)(2,1)} async-done(((bf16[24,768]{1,0:T(8,128)(2,1)}), bf16[768,768]{1,0:T(8,128)(2,1)}) %all-gather.11.cloned.1.call-update) | async-done | bytes 1179664 | tf_op jit(solution)/shard_map/all_gather | solution.py:263
  187.4 11.6 %fusion = (f32[2,12,512]{2,1,0:T(8,128)S(1)}, f32[2,12,512,512]{2,3,1,0:T(8,128)}) fusion(pred[2,512,512]{1,2,0:T(8,128)(4,1)} %broadcast_compare_fusion, bf16[2,512,12,64]{1,0,3,2:T(2,128)(2,1)S(1)} %reshape.162, bf16[2,512,12,64]{1,0,3,2:T(2,128)(2,1)S(1)} %reshape.161), kind=kOutput, calls=%fused_computation.5 | convolution fusion | flops 824168448 | bytes 28884992 | tf_op jit(solution)/shard_map/bqhd,bkhd->bhqk/dot_general | solution.py:67
  199.0 11.2 exponential_reduce_fusion
  210.3 11.6 %fusion.14 = bf16[2,512,12,64]{1,3,2,0:T(8,128)(2,1)S(1)} fusion(bf16[2,512,12,64]{1,0,3,2:T(2,128)(2,1)S(1)} %copy-done.10, f32[2,12,512,512]{2,3,1,0:T(8,128)} %get-tuple-element.101, f32[2,12,512]{2,1,0:T(8,128)S(1)} %log_add_fusion, pred[2,512,512]{1,2,0:T(8,128)(4,1)S(1)} %copy-done.8), kind=kOutput, calls=%fused_computation.55 | convolution fusion | flops 831258624 | bytes 28884992 | tf_op jit(solution)/shard_map/bhqk,bkhd->bqhd/dot_general | solution.py:75
  225.1 10.3 all-gather.13.cloned.1.call-done
  239.8 60.9 %all-gather.15.cloned.1.call-done = bf16[768,3072]{1,0:T(8,128)(2,1)} async-done(((bf16[24,3072]{1,0:T(8,128)(2,1)}), bf16[768,3072]{1,0:T(8,128)(2,1)}) %all-gather.15.cloned.1.call-update) | async-done | bytes 4718608 | tf_op jit(solution)/shard_map/all_gather | solution.py:270
  300.7 10.5 fusion.38
  311.2 54.7 %all-gather.17.cloned.1.call-done = bf16[3072,768]{1,0:T(8,128)(2,1)} async-done(((bf16[96,768]{1,0:T(8,128)(2,1)}), bf16[3072,768]{1,0:T(8,128)(2,1)}) %all-gather.17.cloned.1.call-update) | async-done | bytes 4718608 | tf_op jit(solution)/shard_map/all_gather | solution.py:272
  365.9 12.4 %fusion.44 = (f32[1024]{0:T(1024)S(1)}, f32[1024,768]{1,0:T(8,128)S(1)}) fusion(f32[768]{0:T(1024)S(1)} %convert_element_type.156, bf16[3072,768]{1,0:T(8,128)(2,1)} %all-gather.17.cloned.1.call-done, f32[1024,3072]{1,0:T(8,128)} %fusion.38, f32[3072]{0:T(1024)S(1)} %convert_element_type.154, f32[768]{0:T(1024)S(1)} %convert_element_type.152, ...), kind=kOutput, calls=%fused_computation.91 | convolution fusion | flops 4868799488 | bytes 23626752 | tf_op jit(solution)/shard_map/dot_general | solution.py:25
  384.3 15.8 %convert_reduce_fusion = (f32[3072]{0:T(1024)S(1)}, bf16[1024,3072]{1,0:T(8,128)(2,1)S(1)}) fusion(f32[1024,3072]{1,0:T(8,128)} %fusion.38, f32[3072]{0:T(1024)S(1)} %convert_element_type.154, bf16[1024,768]{1,0:T(8,128)(2,1)S(1)} %get-tuple-element.92, bf16[3072,768]{1,0:T(8,128)(2,1)} %all-gather.17.cloned.1.call-done), kind=kOutput, calls=%fused_computation.16 | convolution fusion | flops 4904186880 | bytes 25190400 | tf_op jit(solution)/shard_map/nd,fd->nf/dot_general | solution.py:139
  424.8 12.1 %convert_reduce_fusion.4 = (f32[12,64]{1,0:T(8,128)S(1)}, bf16[2,512,12,64]{1,3,2,0:T(8,128)(2,1)S(1)}) fusion(f32[2,12,512,512]{2,3,1,0:T(8,128)} %get-tuple-element.101, f32[2,12,512]{2,1,0:T(8,128)S(1)} %log_add_fusion, pred[2,512,512]{1,2,0:T(8,128)(4,1)} %broadcast_compare_fusion, bf16[2,512,12,64]{1,0,3,2:T(2,128)(2,1)} %reshape.164), kind=kOutput, calls=%fused_computation.30 | convolution fusion | flops 832830720 | bytes 28888064 | tf_op jit(solution)/shard_map/bhqk,bqhd->bkhd/dot_general | solution.py:194
  446.1 21.4 %multiply_reduce_fusion = (f32[2,12,512]{2,1,0:T(8,128)S(1)}, f32[2,12,512,512]{2,3,1,0:T(8,128)}) fusion(f32[2,12,512,512]{2,3,1,0:T(8,128)} %get-tuple-element.101, f32[2,12,512]{2,1,0:T(8,128)S(1)} %log_add_fusion, pred[2,512,512]{1,2,0:T(8,128)(4,1)} %broadcast_compare_fusion, bf16[2,512,12,64]{1,0,3,2:T(2,128)(2,1)} %reshape.160, ...), kind=kOutput, calls=%fused_computation.1 | convolution fusion | flops 836751360 | bytes 54099968 | tf_op jit(solution)/shard_map/bqhd,bkhd->bhqk/dot_general | solution.py:191
  467.6 18.0 %multiply_convert_fusion = bf16[2,12,512,512]{2,3,1,0:T(8,128)(2,1)S(1)} fusion(f32[2,12,512,512]{2,3,1,0:T(8,128)} %get-tuple-element.108, f32[2,12,512,512]{2,3,1,0:T(8,128)} %get-tuple-element.101, f32[2,12,512]{2,1,0:T(8,128)S(1)} %get-tuple-element.107, f32[2,12,512]{2,1,0:T(8,128)S(1)} %log_add_fusion, pred[2,512,512]{1,2,0:T(8,128)(4,1)} %broadcast_compare_fusion), kind=kLoop, calls=%fused_computation | loop fusion | flops 37748736 | bytes 63537152 | tf_op jit(solution)/shard_map/convert_element_type | solution.py:198
  499.4 9.1 fusion.17
  518.0 10.7 fusion.36
  530.1 12.8 %fusion.40 = f32[3072,768]{1,0:T(8,128)} fusion(bf16[1024,768]{1,0:T(8,128)(2,1)S(1)} %copy-done.19, f32[1024,3072]{1,0:T(8,128)} %fusion.38, f32[3072]{0:T(1024)S(1)} %convert_element_type.154), kind=kOutput, calls=%fused_computation.87 | convolution fusion | flops 4863295488 | bytes 23605248 | tf_op jit(solution)/shard_map/nf,nd->fd/dot_general | solution.py:138
  544.8 40.6 %all-reduce.18 = (f32[768]{0:T(1024)S(1)}, f32[768]{0:T(1024)S(1)}, f32[768]{0:T(1024)S(1)}, f32[768]{0:T(1024)S(1)}, f32[768]{0:T(1024)S(1)}, /*index=5*/f32[30...) all-reduce(f32[768]{0:T(1024)S(1)} %reduce_sum.191, ...), channel_id=3, replica_groups=mesh['dp'=2,'fsdp'=16] {'dp','fsdp'}, use_global_device_ids=true, to_apply=%region_13.14.clone | all-reduce | flops 9216 | bytes 73728
  599.5 28.4 %reduce-scatter.23.cloned.1.call-done = f32[24,768]{1,0:T(8,128)} async-done(((f32[768,768]{1,0:T(8,128)}), f32[24,768]{1,0:T(8,128)}) %reduce-scatter.23.cloned.1.call-update) | async-done | bytes 73744
  627.9 103.9 %reduce-scatter.19.cloned.1.call-done = f32[24,768]{1,0:T(8,128)} async-done(((f32[768,768]{1,0:T(8,128)}), f32[24,768]{1,0:T(8,128)}) %reduce-scatter.19.cloned.1.call-update) | async-done | bytes 73744
  731.8 104.7 %reduce-scatter.21.cloned.1.call-done = f32[24,768]{1,0:T(8,128)} async-done(((f32[768,768]{1,0:T(8,128)}), f32[24,768]{1,0:T(8,128)}) %reduce-scatter.21.cloned.1.call-update) | async-done | bytes 73744
  836.5 141.0 %reduce-scatter.15.cloned.1.call-done = f32[24,3072]{1,0:T(8,128)} async-done(((f32[768,3072]{1,0:T(8,128)}), f32[24,3072]{1,0:T(8,128)}) %reduce-scatter.15.cloned.1.call-update) | async-done | bytes 294928 | tf_op jit(solution)/shard_map/reduce_scatter | solution.py:320
  977.5 142.0 %reduce-scatter.17.cloned.1.call-done = f32[96,768]{1,0:T(8,128)} async-done(((f32[3072,768]{1,0:T(8,128)}), f32[96,768]{1,0:T(8,128)}) %reduce-scatter.17.cloned.1.call-update) | async-done | bytes 294928 | tf_op jit(solution)/shard_map/reduce_scatter | solution.py:322
  (174 shorter events, 127.1 us)
Async XLA Ops:
  7.2 60.7 %all-gather.9.cloned.1.call-start = ((), (), s32[]{:S(2)}) async-start(), calls=%async_computation.7 | async-start | bytes 1216512 | tf_op jit(solution)/shard_map/all_gather | solution.py:261
  7.9 115.9 %all-gather.7.cloned.1.call-start = ((), (), s32[]{:S(2)}) async-start(), calls=%async_computation.6 | async-start | bytes 1216512 | tf_op jit(solution)/shard_map/all_gather | solution.py:264
  8.7 171.0 %all-gather.11.cloned.1.call-start = ((), (), s32[]{:S(2)}) async-start(), calls=%async_computation.8 | async-start | bytes 1216512 | tf_op jit(solution)/shard_map/all_gather | solution.py:263
  9.4 226.0 %all-gather.13.cloned.1.call-start = ((), (), s32[]{:S(2)}) async-start(), calls=%async_computation.9 | async-start | bytes 1216512 | tf_op jit(solution)/shard_map/all_gather | solution.py:266
  10.0 290.7 %all-gather.15.cloned.1.call-start = ((), (), s32[]{:S(2)}) async-start(), calls=%async_computation.10 | async-start | bytes 4866048 | tf_op jit(solution)/shard_map/all_gather | solution.py:270
  10.6 355.3 %all-gather.17.cloned.1.call-start = ((), (), s32[]{:S(2)}) async-start(), calls=%async_computation.11 | async-start | bytes 4866048 | tf_op jit(solution)/shard_map/all_gather | solution.py:272
  11.1 588.3 %reduce-scatter.13.cloned.1.call-start = ((), (), s32[]{:S(2)}) async-start(), calls=%async_computation.12 | async-start | bytes 2433024 | tf_op jit(solution)/shard_map/reduce_scatter | solution.py:316
  73.0 114.4 %copy-start.5 = (bf16[2,512,12,64]{1,0,3,2:T(2,128)(2,1)}, bf16[2,512,12,64]{1,0,3,2:T(2,128)(2,1)S(1)}, u32[]{:S(2)}) copy-start(bf16[2,512,12,64]{1,0,3,2:T(2,128)(2,1)S(1)} %reshape.161) | copy-start | bytes 4718596
  187.4 11.7 %copy-start.3 = (bf16[2,512,12,64]{1,0,3,2:T(2,128)(2,1)}, bf16[2,512,12,64]{1,0,3,2:T(2,128)(2,1)S(1)}, u32[]{:S(2)}) copy-start(bf16[2,512,12,64]{1,0,3,2:T(2,128)(2,1)S(1)} %reshape.162) | copy-start | bytes 4718596
  187.4 11.7 %copy-start.8 = (pred[2,512,512]{1,2,0:T(8,128)(4,1)S(1)}, pred[2,512,512]{1,2,0:T(8,128)(4,1)}, u32[]{:S(2)}) copy-start(pred[2,512,512]{1,2,0:T(8,128)(4,1)} %broadcast_compare_fusion) | copy-start | bytes 1572868
  199.0 11.2 copy-start.10
  383.9 16.2 %slice-start = ((s8[4718592]{0:T(1024)(128)(4,1)}), s8[4194304]{0:T(1024)(128)(4,1)S(1)}, s32[]{:S(2)}) async-start(s8[4718592]{0:T(1024)(128)(4,1)} %bitcast.110), calls=%async_computation.18 | async-start | bytes 8388608
  384.3 15.8 %copy-start.18 = (bf16[1024,768]{1,0:T(8,128)(2,1)}, bf16[1024,768]{1,0:T(8,128)(2,1)S(1)}, u32[]{:S(2)}) copy-start(bf16[1024,768]{1,0:T(8,128)(2,1)S(1)} %get-tuple-element.92) | copy-start | bytes 4718596
  384.3 15.8 %slice-start.1 = ((s8[4718592]{0:T(1024)(128)(4,1)}), s8[524288]{0:T(1024)(128)(4,1)S(1)}, s32[]{:S(2)}) async-start(s8[4718592]{0:T(1024)(128)(4,1)} %bitcast.110), calls=%async_computation.19 | async-start | bytes 1048576
  400.1 6.1 copy-start.9
  424.7 203.1 %reduce-scatter.23.cloned.1.call-start = ((), (), s32[]{:S(2)}) async-start(), calls=%async_computation.17 | async-start | bytes 2433024
  436.9 3.3 copy-start.23
  467.6 264.3 %reduce-scatter.19.cloned.1.call-start = ((), (), s32[]{:S(2)}) async-start(), calls=%async_computation.15 | async-start | bytes 2433024
  467.6 18.0 %copy-start.4 = (bf16[2,512,12,64]{1,0,3,2:T(2,128)(2,1)S(1)}, bf16[2,512,12,64]{1,0,3,2:T(2,128)(2,1)}, u32[]{:S(2)}) copy-start(bf16[2,512,12,64]{1,0,3,2:T(2,128)(2,1)} %copy-done.3) | copy-start | bytes 4718596
  485.6 4.6 copy-start
  499.3 337.1 %reduce-scatter.21.cloned.1.call-start = ((), (), s32[]{:S(2)}) async-start(), calls=%async_computation.16 | async-start | bytes 2433024
  517.6 459.9 %reduce-scatter.15.cloned.1.call-start = ((), (), s32[]{:S(2)}) async-start(), calls=%async_computation.13 | async-start | bytes 9732096 | tf_op jit(solution)/shard_map/reduce_scatter | solution.py:320
  528.7 590.7 %reduce-scatter.17.cloned.1.call-start = ((), (), s32[]{:S(2)}) async-start(), calls=%async_computation.14 | async-start | bytes 9732096 | tf_op jit(solution)/shard_map/reduce_scatter | solution.py:322
  543.0 47.7 %copy-start.14 = (bf16[96,8,2,512]{3,1,2,0:T(8,128)(2,1)S(1)}, bf16[96,8,2,512]{3,1,2,0:T(8,128)(2,1)}, u32[]{:S(2)}) copy-start(bf16[96,8,2,512]{3,1,2,0:T(8,128)(2,1)} %copy-done.13) | copy-start | bytes 4718596
  (17 other events, 34.9 us)
Sparse Core Ops, SparseCore 0:
  10.9 56.9 all-gather.8
  70.7 53.0 all-gather.6
  126.8 52.9 all-gather.10
  182.4 52.9 all-gather.12
  238.1 62.5 all-gather.14
  303.4 62.3 all-gather.16
  424.8 97.8 reduce-scatter.12
  529.4 98.3 reduce-scatter.22
  633.7 98.0 reduce-scatter.18
  738.4 98.0 reduce-scatter.20
  842.9 134.4 reduce-scatter.14
  984.8 134.6 reduce-scatter.16
where the time goes:
time: 1140 us; the launch traced here: 1130 us
  waiting for transfers between devices  753 us (66%)
  matrix products  174 us (15%)
  blocking collectives  83 us (7%)
  local copies, waits for them, and re-layouts  62.1 us (5%)
  other arithmetic  39 us (3%)
  between operations  15 us (1%)
    unnamed x15, waiting for transfers between devices  241 us
    reduce_scatter x1, waiting for transfers between devices, on_device(): lax.psum_scatter(d_w_outer, ('dp', 'fsdp'), scatter_dimension=0, tiled=True)  142 us
    reduce_scatter x1, waiting for transfers between devices, on_device(): lax.psum_scatter(d_w_inner, ('dp', 'fsdp'), scatter_dimension=0, tiled=True)  141 us
    unnamed x2, blocking collectives  83 us
    all_gather x1, waiting for transfers between devices, on_device(): lax.all_gather(w_inner, ('dp', 'fsdp'), axis=0, tiled=True)  60.9 us
    all_gather x1, waiting for transfers between devices, on_device(): lax.all_gather(w_outer, ('dp', 'fsdp'), axis=0, tiled=True)  54.7 us
    all_gather x1, waiting for transfers between devices, on_device(): lax.all_gather(w_value, ('dp', 'fsdp'), axis=0, tiled=True)  50.9 us
    all_gather x1, waiting for transfers between devices, on_device(): lax.all_gather(w_key, ('dp', 'fsdp'), axis=0, tiled=True)  47.5 us
  transfers between devices with their start and end apart: 12, of which 11 were waited for; matrix products, arithmetic and copies ran while one was open for 18% of the time, Pallas kernels for 0%

commit v1 on v0

--- a/solution.py
+++ b/solution.py
@@ -236,6 +236,72 @@
     )
 
 
+AXES = ("dp", "fsdp")
+MATRICES = (0, 2, 3, 5, 9, 11)
+VECTORS = (1, 4, 6, 7, 8, 10, 12, 13, 14)
+
+
+def to_rows(array, lead):
+    rows, columns = array.shape[-2:]
+    if columns == D:
+        return array
+    blocks = [array[..., i : i + D] for i in range(0, columns, D)]
+    return jnp.concatenate(blocks, axis=lead)
+
+
+def gather_params(params):
+    pieces = [to_rows(params[i], 0) for i in MATRICES]
+    vector = jnp.concatenate([params[i] for i in VECTORS])
+    pieces.append(jnp.pad(vector, (0, -vector.size % D)).reshape(-1, D))
+    packed = jnp.concatenate(pieces, axis=0)
+    whole = lax.all_gather(packed, AXES, axis=0, tiled=False)
+    count = whole.shape[0]
+    full = [None] * len(params)
+    start = 0
+    for i in MATRICES:
+        rows, columns = params[i].shape
+        blocks = []
+        for _ in range(columns // D):
+            blocks.append(whole[:, start : start + rows].reshape(count * rows, D))
+            start += rows
+        full[i] = jnp.concatenate(blocks, axis=1)
+    vectors = whole[:, start:].reshape(count, -1)
+    start = 0
+    for i in VECTORS:
+        size = params[i].size
+        full[i] = vectors[:, start : start + size].reshape(-1)
+        start += size
+    return tuple(full)
+
+
+def scatter_grads(grads):
+    count = lax.axis_size(AXES)
+    low = [grad.astype(jnp.bfloat16) for grad in grads]
+    pieces = [to_rows(low[i].reshape(count, -1, low[i].shape[1]), 1) for i in MATRICES]
+    vector = jnp.concatenate([low[i].reshape(count, -1) for i in VECTORS], axis=1)
+    vector = jnp.pad(vector, ((0, 0), (0, -vector.shape[1] % D)))
+    pieces.append(vector.reshape(count, -1, D))
+    packed = jnp.concatenate(pieces, axis=1)
+    mine = lax.psum_scatter(packed, AXES, scatter_dimension=0, tiled=False)
+    mine = mine.astype(jnp.float32)
+    shards = [None] * len(grads)
+    start = 0
+    for i in MATRICES:
+        rows, columns = grads[i].shape[0] // count, grads[i].shape[1]
+        blocks = []
+        for _ in range(columns // D):
+            blocks.append(mine[start : start + rows])
+            start += rows
+        shards[i] = jnp.concatenate(blocks, axis=1)
+    vectors = mine[start:].reshape(-1)
+    start = 0
+    for i in VECTORS:
+        size = grads[i].size // count
+        shards[i] = vectors[start : start + size]
+        start += size
+    return shards
+
+
 def on_device(
     block_input,
     segment_ids,
@@ -257,42 +323,11 @@
     shift_two,
 ):
     same_segment = segment_ids[:, :, None] == segment_ids[:, None, :]
-    params = (
-        lax.all_gather(w_query, ("dp", "fsdp"), axis=0, tiled=True),
-        lax.all_gather(b_query, ("dp", "fsdp"), axis=0, tiled=True),
-        lax.all_gather(w_key, ("dp", "fsdp"), axis=0, tiled=True),
-        lax.all_gather(w_value, ("dp", "fsdp"), axis=0, tiled=True),
-        lax.all_gather(b_value, ("dp", "fsdp"), axis=0, tiled=True),
-        lax.all_gather(w_out, ("dp", "fsdp"), axis=0, tiled=True),
-        lax.all_gather(b_out, ("dp", "fsdp"), axis=0, tiled=True),
-        lax.all_gather(gain_one, ("dp", "fsdp"), axis=0, tiled=True),
-        lax.all_gather(shift_one, ("dp", "fsdp"), axis=0, tiled=True),
-        lax.all_gather(w_inner, ("dp", "fsdp"), axis=0, tiled=True),
-        lax.all_gather(b_inner, ("dp", "fsdp"), axis=0, tiled=True),
-        lax.all_gather(w_outer, ("dp", "fsdp"), axis=0, tiled=True),
-        lax.all_gather(b_outer, ("dp", "fsdp"), axis=0, tiled=True),
-        lax.all_gather(gain_two, ("dp", "fsdp"), axis=0, tiled=True),
-        lax.all_gather(shift_two, ("dp", "fsdp"), axis=0, tiled=True),
+    params = gather_params(
+        (w_query, b_query, w_key, w_value, b_value, w_out, b_out, gain_one, shift_one)
+        + (w_inner, b_inner, w_outer, b_outer, gain_two, shift_two)
     )
     result, kept = forward(block_input, same_segment, params)
-    params = (
-        lax.all_gather(w_query, ("dp", "fsdp"), axis=0, tiled=True),
-        lax.all_gather(b_query, ("dp", "fsdp"), axis=0, tiled=True),
-        lax.all_gather(w_key, ("dp", "fsdp"), axis=0, tiled=True),
-        lax.all_gather(w_value, ("dp", "fsdp"), axis=0, tiled=True),
-        lax.all_gather(b_value, ("dp", "fsdp"), axis=0, tiled=True),
-        lax.all_gather(w_out, ("dp", "fsdp"), axis=0, tiled=True),
-        lax.all_gather(b_out, ("dp", "fsdp"), axis=0, tiled=True),
-        lax.all_gather(gain_one, ("dp", "fsdp"), axis=0, tiled=True),
-        lax.all_gather(shift_one, ("dp", "fsdp"), axis=0, tiled=True),
-        lax.all_gather(w_inner, ("dp", "fsdp"), axis=0, tiled=True),
-        lax.all_gather(b_inner, ("dp", "fsdp"), axis=0, tiled=True),
-        lax.all_gather(w_outer, ("dp", "fsdp"), axis=0, tiled=True),
-        lax.all_gather(b_outer, ("dp", "fsdp"), axis=0, tiled=True),
-        lax.all_gather(gain_two, ("dp", "fsdp"), axis=0, tiled=True),
-        lax.all_gather(shift_two, ("dp", "fsdp"), axis=0, tiled=True),
-    )
-    result_again, kept = forward(block_input, same_segment, params)
     d_normed, ffn_terms = backward_ffn(cotangent, params, kept)
     d_w_inner, d_b_inner, d_w_outer, d_b_outer, d_gain_two, d_shift_two = ffn_terms
     d_input, attention_terms = backward_attention(block_input, same_segment, d_normed, params, kept)
@@ -307,22 +342,9 @@
         d_gain_one,
         d_shift_one,
     ) = attention_terms
-    shards = (
-        lax.psum_scatter(d_w_query, ("dp", "fsdp"), scatter_dimension=0, tiled=True),
-        lax.psum_scatter(d_b_query, ("dp", "fsdp"), scatter_dimension=0, tiled=True),
-        lax.psum_scatter(d_w_key, ("dp", "fsdp"), scatter_dimension=0, tiled=True),
-        lax.psum_scatter(d_w_value, ("dp", "fsdp"), scatter_dimension=0, tiled=True),
-        lax.psum_scatter(d_b_value, ("dp", "fsdp"), scatter_dimension=0, tiled=True),
-        lax.psum_scatter(d_w_out, ("dp", "fsdp"), scatter_dimension=0, tiled=True),
-        lax.psum_scatter(d_b_out, ("dp", "fsdp"), scatter_dimension=0, tiled=True),
-        lax.psum_scatter(d_gain_one, ("dp", "fsdp"), scatter_dimension=0, tiled=True),
-        lax.psum_scatter(d_shift_one, ("dp", "fsdp"), scatter_dimension=0, tiled=True),
-        lax.psum_scatter(d_w_inner, ("dp", "fsdp"), scatter_dimension=0, tiled=True),
-        lax.psum_scatter(d_b_inner, ("dp", "fsdp"), scatter_dimension=0, tiled=True),
-        lax.psum_scatter(d_w_outer, ("dp", "fsdp"), scatter_dimension=0, tiled=True),
-        lax.psum_scatter(d_b_outer, ("dp", "fsdp"), scatter_dimension=0, tiled=True),
-        lax.psum_scatter(d_gain_two, ("dp", "fsdp"), scatter_dimension=0, tiled=True),
-        lax.psum_scatter(d_shift_two, ("dp", "fsdp"), scatter_dimension=0, tiled=True),
+    shards = scatter_grads(
+        (d_w_query, d_b_query, d_w_key, d_w_value, d_b_value, d_w_out, d_b_out, d_gain_one)
+        + (d_shift_one, d_w_inner, d_b_inner, d_w_outer, d_b_outer, d_gain_two, d_shift_two)
     )
     return (
         result,

time: 1140 us -> 578 us (0.51)
  waiting for transfers between devices: 753 us -> 258 us
  blocking collectives: 83 us -> 0 us
  local copies, waits for them, and re-layouts: 62.1 us -> 73.6 us
    unnamed x15 -> x2, waiting for transfers between devices: 241 us -> 0.03 us
    reduce_scatter x3 -> x1, waiting for transfers between devices: 283 us -> 155 us  [scatter_grads(): mine = lax.psum_scatter(packed, AXES, scatter_dimension=0, tiled=False)]
    all_gather x6 -> x1, waiting for transfers between devices: 229 us -> 103 us  [gather_params(): whole = lax.all_gather(packed, AXES, axis=0, tiled=False)]
    unnamed x2 -> x0, blocking collectives: 83 us -> none
    slice x0 -> x7, local copies, waits for them, and re-layouts: none -> 13.1 us  [the longest x2 9.41 us: gather_params(): blocks.append(whole[:, start:start + rows].reshape(count * rows, D))]
    unnamed x92 -> x95, local copies, waits for them, and re-layouts: 38.5 us -> 27 us
  transfers between devices with their start and end apart: 12 -> 2, of which waited for: 11 -> 2; matrix products, arithmetic and copies ran while one was open for 18% -> 2% of each run, Pallas kernels for 0% -> 0%
where the time goes in v1:
time: 578 us; the launch traced here: 569 us
  waiting for transfers between devices  258 us (45%)
  matrix products  176 us (30%)
  local copies, waits for them, and re-layouts  73.6 us (13%)
  other arithmetic  45.7 us (8%)
  between operations  15.2 us (3%)
    reduce_scatter x1, waiting for transfers between devices, scatter_grads(): mine = lax.psum_scatter(packed, AXES, scatter_dimension=0, tiled=False)  155 us
    all_gather x1, waiting for transfers between devices, gather_params(): whole = lax.all_gather(packed, AXES, axis=0, tiled=False)  103 us
    dot_general x6, matrix products, matmul(): return jnp.dot(left, right, preferred_element_type=jnp.float32)  33.6 us
    unnamed x95, local copies, waits for them, and re-layouts  27 us
    convert_element_type x1, other arithmetic, backward_attention(): d_scores = d_scores.astype(jnp.bfloat16)  21.6 us
    dot_general x1, matrix products, backward_attention(): jnp.einsum('bqhd,bkhd->bhqk', d_context, value_heads, preferred_element_t...  21 us
    dot_general x1, matrix products, backward_ffn(): jnp.einsum('nd,fd->nf', d_branch, w_outer, preferred_element_type=jnp.flo...  16.3 us
    dot_general x1, matrix products, backward_attention(): jnp.einsum('bhqk,bqhd->bkhd', probs.astype(jnp.bfloat16), d_context, pref...  12.7 us
  transfers between devices with their start and end apart: 2, of which 2 were waited for; matrix products, arithmetic and copies ran while one was open for 2% of the time, Pallas kernels for 0%

profile of v1, /device:TPU:0, one launch (start us, length us, event | category | flops | bytes accessed | tf_op | source)
XLA Modules:
  0.0 569.3 jit_solution(6436784811155037542)
XLA Ops:
  13.4 6.1 %concatenate.18 = bf16[288]{0:T(512)(128)(2,1)S(1)} concatenate(bf16[24]{0:T(256)(128)(2,1)} %param.22, bf16[24]{0:T(256)(128)(2,1)} %param.25, bf16[24]{0:T(256)(128)(2,1)} %param.27, bf16[24]{0:T(256)(128)(2,1)} %param.28, bf16[24]{0:T(256)(128)(2,1)} %param.29, bf16[96]{0:T(256)(128)(2,1)} %param.31, bf16[24]{0:T(256)(128)(2,1)} %param.33, bf16[24]{0:T(256)(128)(2,1)} %param.34, ...), dimensions={0} | concatenate | bytes 1152 | tf_op jit(solution)/shard_map/concatenate | solution.py:254
  25.6 103.4 %all-gather.4.cloned.1.call-done = bf16[32,289,768]{2,1,0:T(8,128)(2,1)} async-done(((bf16[1,289,768]{2,1,0:T(8,128)(2,1)}), bf16[32,289,768]{2,1,0:T(8,128)(2,1)}) %all-gather.4.cloned.1.call-update) | async-done | bytes 14204944 | tf_op jit(solution)/shard_map/all_gather | solution.py:257
  131.0 6.8 %fusion.48 = (bf16[32,24,768]{2,1,0:T(8,128)(2,1)}, bf16[32,24,768]{2,1,0:T(8,128)(2,1)}, bf16[32,24,768]{2,1,0:T(8,128)(2,1)}, bf16[32,24,768]{2,1,0:T(8,128)(2...) fusion(bf16[32,289,768]{2,1,0:T(8,128)(2,1)} %all-gather.4.clon, ...), kind=kLoop, calls=%fused_computation.144 | loop fusion | bytes 18874368 | tf_op jit(solution)/shard_map/slice | solution.py:265
  144.4 4.6 fusion.19
  149.0 4.0 reshape.325
  153.0 4.0 fusion.18
  159.9 11.6 %fusion = (f32[2,12,512]{2,1,0:T(8,128)S(1)}, f32[2,12,512,512]{2,3,1,0:T(8,128)}) fusion(pred[2,512,512]{1,2,0:T(8,128)(4,1)} %broadcast_compare_fusion, bf16[2,512,12,64]{1,0,3,2:T(2,128)(2,1)S(1)} %reshape.329, bf16[2,512,12,64]{1,0,3,2:T(2,128)(2,1)S(1)} %reshape.327), kind=kOutput, calls=%fused_computation.5 | convolution fusion | flops 824168448 | bytes 28884992 | tf_op jit(solution)/shard_map/bqhd,bkhd->bhqk/dot_general | solution.py:67
  171.5 11.2 %exponential_reduce_fusion = f32[2,12,512]{2,1,0:T(8,128)S(1)} fusion(f32[2,12,512,512]{2,3,1,0:T(8,128)} %get-tuple-element.66, f32[2,12,512]{2,1,0:T(8,128)S(1)} %get-tuple-element.65, pred[2,512,512]{1,2,0:T(8,128)(4,1)S(1)} %copy-done.5), kind=kLoop, calls=%fused_computation.3 | loop fusion | flops 25153536 | bytes 25788416 | tf_op jit(solution)/shard_map/reduce_sum | solution.py:72
  182.7 11.6 %fusion.14 = bf16[2,512,12,64]{1,3,2,0:T(8,128)(2,1)S(1)} fusion(bf16[2,512,12,64]{1,0,3,2:T(2,128)(2,1)S(1)} %copy-done.7, f32[2,12,512,512]{2,3,1,0:T(8,128)} %get-tuple-element.66, f32[2,12,512]{2,1,0:T(8,128)S(1)} %log_add_fusion, pred[2,512,512]{1,2,0:T(8,128)(4,1)S(1)} %copy-done.5), kind=kOutput, calls=%fused_computation.53 | convolution fusion | flops 831258624 | bytes 28884992 | tf_op jit(solution)/shard_map/bhqk,bkhd->bqhd/dot_general | solution.py:75
  199.7 9.7 %fusion.31 = f32[1024,3072]{1,0:T(8,128)} fusion(bf16[768,768]{1,0:T(8,128)(2,1)S(1)} %bitcast.183, bf16[768,768]{1,0:T(8,128)(2,1)S(1)} %bitcast.185, bf16[768,768]{1,0:T(8,128)(2,1)S(1)} %bitcast.187, bf16[768,768]{1,0:T(8,128)(2,1)S(1)} %bitcast.181, f32[1024,768]{1,0:T(8,128)S(1)} %get-tuple-element.68, f32[768]{0:T(1024)S(1)} %reshape.358, ...), kind=kOutput, calls=%fused_computation.75 | convolution fusion | flops 4854644736 | bytes 20461568 | tf_op jit(solution)/shard_map/dot_general | solution.py:25
  212.1 10.9 %fusion.50 = (f32[1024]{0:T(1024)S(1)}, f32[1024,768]{1,0:T(8,128)S(1)}) fusion(f32[768]{0:T(1024)S(1)} %reshape.360, bf16[3072,768]{1,0:T(8,128)(2,1)S(1)} %bitcast.165, f32[1024,3072]{1,0:T(8,128)} %fusion.31, f32[3072]{0:T(1024)S(1)} %reshape.359, f32[768]{0:T(1024)S(1)} %reshape.358, f32[768]{0:T(1024)S(1)} %reshape.357, f32[1024]{0:T(1024)S(1)} %fusion.34, ...), kind=kOutput, calls=%fused_computation.146 | convolution fusion | flops 4868799488 | bytes 23626752 | tf_op jit(solution)/shard_map/dot_general | solution.py:25
  228.7 16.3 %fusion.53 = (bf16[3072]{0:T(1024)(128)(2,1)S(1)}, bf16[1024,3072]{1,0:T(8,128)(2,1)}) fusion(f32[1024,3072]{1,0:T(8,128)} %fusion.31, f32[3072]{0:T(1024)S(1)} %reshape.359, bf16[1024,768]{1,0:T(8,128)(2,1)S(1)} %get-tuple-element.23, bf16[3072,768]{1,0:T(8,128)(2,1)S(1)} %bitcast.166), kind=kOutput, calls=%fused_computation.149 | convolution fusion | flops 4901041152 | bytes 25184256 | tf_op jit(solution)/shard_map/nd,fd->nf/dot_general | solution.py:139
  245.0 12.7 %convolution_convert_fusion = bf16[3072,768]{1,0:T(8,128)(2,1)} fusion(bf16[1024,768]{1,0:T(8,128)(2,1)S(1)} %get-tuple-element.23, f32[1024,3072]{1,0:T(8,128)} %fusion.31, f32[3072]{0:T(1024)S(1)} %reshape.359), kind=kOutput, calls=%fused_computation.17 | convolution fusion | flops 4865654784 | bytes 18886656 | tf_op jit(solution)/shard_map/nf,nd->fd/dot_general | solution.py:138
  257.7 8.8 %multiply_reduce_fusion.1 = (bf16[768]{0:T(1024)(128)(2,1)S(1)}, f32[1024]{0:T(1024)S(1)}, bf16[768]{0:T(1024)(128)(2,1)S(1)}, f32[1024,768]{1,0:T(8,128)S(1)}) fusion(f32[1024,768]{1,0:T(8,128)S(1)} %get-tuple-element.68, f32[1024]{0:T(1024)S(1)} %fusion.34, f32[1024]{0:T(1024)S(1)} %broadcast_multiply_fusion.1, f32[768]{0:T(1024)S(1)} %reshape.357, ...), kind=kOutput, calls=%fused_computation.28 | convolution fusion | flops 4858573824 | bytes 20469760 | tf_op jit(solution)/shard_map/nf,df->nd/dot_general | solution.py:144
  266.5 10.0 %convolution_convert_fusion.1 = bf16[768,3072]{1,0:T(8,128)(2,1)} fusion(bf16[1024,3072]{1,0:T(8,128)(2,1)} %get-tuple-element.79, f32[1024,768]{1,0:T(8,128)S(1)} %get-tuple-element.68, f32[768]{0:T(1024)S(1)} %reshape.358, f32[768]{0:T(1024)S(1)} %reshape.357, f32[1024]{0:T(1024)S(1)} %fusion.34, f32[1024]{0:T(1024)S(1)} %broadcast_multiply_fusion.1), kind=kOutput, calls=%fused_computation.18 | convolution fusion | flops 4838129664 | bytes 14170112 | tf_op jit(solution)/shard_map/nd,nf->df/dot_general | solution.py:143
  286.1 3.8 reshape.337
  289.9 12.7 %fusion.52 = (bf16[12,64]{1,0:T(8,128)(2,1)S(1)}, bf16[2,512,12,64]{1,3,2,0:T(8,128)(2,1)}) fusion(f32[2,12,512,512]{2,3,1,0:T(8,128)} %get-tuple-element.66, f32[2,12,512]{2,1,0:T(8,128)S(1)} %log_add_fusion, pred[2,512,512]{1,2,0:T(8,128)(4,1)} %broadcast_compare_fusion, bf16[2,512,12,64]{1,0,3,2:T(2,128)(2,1)} %reshape.337), kind=kOutput, calls=%fused_computation.148 | convolution fusion | flops 832044288 | bytes 28886528 | tf_op jit(solution)/shard_map/bhqk,bqhd->bkhd/dot_general | solution.py:194
  302.7 21.0 %multiply_reduce_fusion = (f32[2,12,512]{2,1,0:T(8,128)S(1)}, f32[2,12,512,512]{2,3,1,0:T(8,128)}) fusion(f32[2,12,512,512]{2,3,1,0:T(8,128)} %get-tuple-element.66, f32[2,12,512]{2,1,0:T(8,128)S(1)} %log_add_fusion, pred[2,512,512]{1,2,0:T(8,128)(4,1)} %broadcast_compare_fusion, bf16[2,512,12,64]{1,0,3,2:T(2,128)(2,1)} %reshape.325, ...), kind=kOutput, calls=%fused_computation.1 | convolution fusion | flops 836751360 | bytes 54099968 | tf_op jit(solution)/shard_map/bqhd,bkhd->bhqk/dot_general | solution.py:191
  323.7 21.6 %multiply_convert_fusion = bf16[2,12,512,512]{2,3,1,0:T(8,128)(2,1)} fusion(f32[2,12,512,512]{2,3,1,0:T(8,128)} %get-tuple-element.73, f32[2,12,512,512]{2,3,1,0:T(8,128)} %get-tuple-element.66, f32[2,12,512]{2,1,0:T(8,128)S(1)} %get-tuple-element.72, f32[2,12,512]{2,1,0:T(8,128)S(1)} %log_add_fusion, pred[2,512,512]{1,2,0:T(8,128)(4,1)} %broadcast_compare_fusion), kind=kLoop, calls=%fused_computation | loop fusion | flops 37748736 | bytes 63537152 | tf_op jit(solution)/shard_map/convert_element_type | solution.py:198
  345.4 9.7 %fusion.17 = bf16[2,512,12,64]{1,3,2,0:T(8,128)(2,1)} fusion(bf16[2,12,512,512]{2,3,1,0:T(8,128)(2,1)} %multiply_convert_fusion, bf16[2,512,12,64]{1,0,3,2:T(2,128)(2,1)S(1)} %copy-done.3), kind=kOutput, calls=%fused_computation.56 | convolution fusion | flops 806879232 | bytes 15728640 | tf_op jit(solution)/shard_map/bhqk,bqhd->bkhd/dot_general | solution.py:205
  355.1 7.9 %fusion.51 = (bf16[12,64]{1,0:T(8,128)(2,1)S(1)}, bf16[2,512,12,64]{1,3,2,0:T(8,128)(2,1)}) fusion(bf16[2,12,512,512]{2,3,1,0:T(8,128)(2,1)} %multiply_convert_fusion, bf16[2,512,12,64]{1,0,3,2:T(2,128)(2,1)S(1)} %copy-done.1), kind=kOutput, calls=%fused_computation.147 | convolution fusion | flops 807664896 | bytes 15730176 | tf_op jit(solution)/shard_map/bhqk,bkhd->bqhd/dot_general | solution.py:201
  374.4 3.4 convolution_convert_fusion.8
  394.3 3.4 fusion.55
  402.7 154.8 %reduce-scatter.2.cloned.1.call-done = bf16[1,289,768]{2,1,0:T(8,128)(2,1)} async-done(((bf16[32,289,768]{2,1,0:T(8,128)(2,1)}), bf16[1,289,768]{2,1,0:T(8,128)(2,1)}) %reduce-scatter.2.cloned.1.call-update) | async-done | bytes 443920 | tf_op jit(solution)/shard_map/reduce_scatter | solution.py:285
  (167 shorter events, 84.0 us)
Async XLA Ops:
  7.2 121.8 %all-gather.4.cloned.1.call-start = ((), (), s32[]{:S(2)}) async-start(), calls=%async_computation.2 | async-start | bytes 15003648 | tf_op jit(solution)/shard_map/all_gather | solution.py:257
  21.2 536.2 %reduce-scatter.2.cloned.1.call-start = ((), (), s32[]{:S(2)}) async-start(), calls=%async_computation.1 | async-start | bytes 15003648 | tf_op jit(solution)/shard_map/reduce_scatter | solution.py:285
  131.0 7.8 %copy-start.28 = (bf16[2,512,768]{2,1,0:T(8,128)(2,1)S(1)}, bf16[2,512,768]{2,1,0:T(8,128)(2,1)}, u32[]{:S(2)}) copy-start(bf16[2,512,768]{2,1,0:T(8,128)(2,1)} %param.18) | copy-start | bytes 4718596
  137.8 6.6 %copy-start.11 = (bf16[32,24,768]{2,1,0:T(8,128)(2,1)}, bf16[32,24,768]{2,1,0:T(8,128)(2,1)S(1)}, u32[]{:S(2)}) copy-start(bf16[32,24,768]{2,1,0:T(8,128)(2,1)S(1)} %get-tuple-element.37) | copy-start | bytes 3538948
  144.4 15.5 %copy-start.2 = (bf16[2,512,12,64]{1,0,3,2:T(2,128)(2,1)}, bf16[2,512,12,64]{1,0,3,2:T(2,128)(2,1)S(1)}, u32[]{:S(2)}) copy-start(bf16[2,512,12,64]{1,0,3,2:T(2,128)(2,1)S(1)} %reshape.327) | copy-start | bytes 4718596
  149.0 4.0 copy-start.17
  159.8 11.7 %copy-start = (bf16[2,512,12,64]{1,0,3,2:T(2,128)(2,1)}, bf16[2,512,12,64]{1,0,3,2:T(2,128)(2,1)S(1)}, u32[]{:S(2)}) copy-start(bf16[2,512,12,64]{1,0,3,2:T(2,128)(2,1)S(1)} %reshape.329) | copy-start | bytes 4718596
  159.9 11.6 %copy-start.5 = (pred[2,512,512]{1,2,0:T(8,128)(4,1)S(1)}, pred[2,512,512]{1,2,0:T(8,128)(4,1)}, u32[]{:S(2)}) copy-start(pred[2,512,512]{1,2,0:T(8,128)(4,1)} %broadcast_compare_fusion) | copy-start | bytes 1572868
  171.5 11.2 %copy-start.7 = (bf16[2,512,12,64]{1,0,3,2:T(2,128)(2,1)S(1)}, bf16[2,512,12,64]{1,0,3,2:T(2,128)(2,1)}, u32[]{:S(2)}) copy-start(bf16[2,512,12,64]{1,0,3,2:T(2,128)(2,1)} %reshape.325) | copy-start | bytes 4718596
  245.0 12.7 %copy-start.23 = (bf16[32,24,768]{2,1,0:T(8,128)(2,1)S(1)}, bf16[32,24,768]{2,1,0:T(8,128)(2,1)}, u32[]{:S(2)}) copy-start(bf16[32,24,768]{2,1,0:T(8,128)(2,1)} %get-tuple-element.33) | copy-start | bytes 3538948
  323.7 21.6 %copy-start.3 = (bf16[2,512,12,64]{1,0,3,2:T(2,128)(2,1)S(1)}, bf16[2,512,12,64]{1,0,3,2:T(2,128)(2,1)}, u32[]{:S(2)}) copy-start(bf16[2,512,12,64]{1,0,3,2:T(2,128)(2,1)} %copy-done.2) | copy-start | bytes 4718596
  345.3 9.8 %copy-start.1 = (bf16[2,512,12,64]{1,0,3,2:T(2,128)(2,1)S(1)}, bf16[2,512,12,64]{1,0,3,2:T(2,128)(2,1)}, u32[]{:S(2)}) copy-start(bf16[2,512,12,64]{1,0,3,2:T(2,128)(2,1)} %copy-done) | copy-start | bytes 4718596
  363.7 4.8 copy-start.30
  368.4 2.5 copy-start.10
  371.0 3.3 copy-start.27
  374.4 3.5 copy-start.6
  377.8 2.3 copy-start.31
  380.2 6.1 %slice-start.2 = ((s8[4718592]{0:T(1024)(128)(4,1)}), s8[524288]{0:T(1024)(128)(4,1)S(1)}, s32[]{:S(2)}) async-start(s8[4718592]{0:T(1024)(128)(4,1)} %bitcast.159), calls=%async_computation.5 | async-start | bytes 1048576
  381.7 3.4 copy-start.24
  381.7 4.6 slice-start.3
  382.8 8.2 %slice-start = ((s8[4718592]{0:T(1024)(128)(4,1)}), s8[4194304]{0:T(1024)(128)(4,1)S(1)}, s32[]{:S(2)}) async-start(s8[4718592]{0:T(1024)(128)(4,1)} %bitcast.156), calls=%async_computation.3 | async-start | bytes 8388608
  386.2 4.7 slice-start.1
  394.3 3.4 copy-start.14
  394.3 3.4 copy-start.16
  (14 other events, 23.0 us)
Sparse Core Ops, SparseCore 0:
  21.4 107.6 all-gather.3
  394.4 163.0 reduce-scatter.1

commit v2 on v1

v2 whole, which is shorter than its diff:
```python
import jax, jax.numpy as jnp
from jax import lax
from jax.experimental import pallas as pl
from jax.experimental.pallas import tpu as pltpu
from jax.sharding import PartitionSpec as P

D = 768
HEADS = 12
HEAD_DIM = 64
SEQ = 512
GROUP = 256
GROUPS = D // GROUP
TILE = 128
MOST = 192
QT = 512
KT = 256
LOW = jnp.bfloat16
F32 = jnp.float32
MIB = 1 << 20


def mm(a, b):
    return lax.dot_general(a, b, (((1,), (0,)), ((), ())), preferred_element_type=F32)


def mm_t(a, b):
    return lax.dot_general(a, b, (((1,), (1,)), ((), ())), preferred_element_type=F32)


def t_mm(a, b):
    return lax.dot_general(a, b, (((0,), (0,)), ((), ())), preferred_element_type=F32)


def near(i, tile):
    lo, hi = i * tile - MOST + 1, (i + 1) * tile + MOST - 1
    lo = max(0, lo // TILE * TILE)
    hi = min(SEQ, -(-hi // TILE) * TILE)
    return slice(lo, hi)


def attention_forward_kernel(
    x_ref, wq_ref, wk_ref, wv_ref, bq_ref, bv_ref, seg_col_ref, seg_row_ref, wo_ref, bo_ref,
    q_ref, k_ref, v_ref, ctx_ref, lse_ref, h1_ref, mask_ref,
):
    group = pl.program_id(1)
    x = x_ref[...]
    q_ref[...] = (mm(x, wq_ref[...]) + bq_ref[...]).astype(LOW)
    k_ref[...] = mm(x, wk_ref[...]).astype(LOW)
    v_ref[...] = (mm(x, wv_ref[...]) + bv_ref[...]).astype(LOW)

    @pl.when(group == 0)
    def _():
        mask_ref[...] = jnp.where(seg_col_ref[...] == seg_row_ref[0], 0.0, -1e30)

    lane = lax.broadcasted_iota(jnp.int32, (1, TILE), 1)
    scale = jnp.asarray(HEAD_DIM**-0.5, LOW)
    for pair in range(GROUP // TILE):
        lanes = slice(pair * TILE, (pair + 1) * TILE)
        for i in range(SEQ // QT):
            rows = slice(i * QT, (i + 1) * QT)
            keys = near(i, QT)
            q_pair = q_ref[rows, lanes] * scale
            v_pair = v_ref[keys, lanes]
            halves = []
            for half in range(2):
                head = 2 * pair + half
                mine = (lane // HEAD_DIM) == half
                scores = mm_t(jnp.where(mine, k_ref[keys, lanes], 0), q_pair)
                scores = scores + mask_ref[keys, rows]
                top = jnp.max(scores, axis=0, keepdims=True)
                weight = jnp.exp(scores - top)
                total = jnp.sum(weight, axis=0, keepdims=True)
                halves.append(t_mm((weight * (1.0 / total)).astype(LOW), v_pair))
                lse_ref[0, 0, head : head + 1, rows] = top + jnp.log(total)
            ctx_ref[rows, lanes] = jnp.where(lane < HEAD_DIM, halves[0], halves[1]).astype(LOW)

    @pl.when(group == 0)
    def _():
        h1_ref[...] = x.astype(F32) + bo_ref[...] + mm(ctx_ref[...], wo_ref[...])

    @pl.when(group > 0)
    def _():
        h1_ref[...] += mm(ctx_ref[...], wo_ref[...])


def attention_forward(x, seg, wq, bq, wk, wv, bv, wo, bo):
    rows = x.shape[0]
    seqs = rows // SEQ
    token = lambda b, g: (b, 0)
    mine = lambda b, g: (b, g)
    column = lambda b, g: (0, g)
    return pl.pallas_call(
        attention_forward_kernel,
        grid=(seqs, GROUPS),
        in_specs=[
            pl.BlockSpec((SEQ, D), token),
            pl.BlockSpec((D, GROUP), column),
            pl.BlockSpec((D, GROUP), column),
            pl.BlockSpec((D, GROUP), column),
            pl.BlockSpec((1, GROUP), column),
            pl.BlockSpec((1, GROUP), column),
            pl.BlockSpec((SEQ, 1), token),
            pl.BlockSpec((1, 1, SEQ), lambda b, g: (b, 0, 0)),
            pl.BlockSpec((GROUP, D), lambda b, g: (g, 0)),
            pl.BlockSpec((1, D), lambda b, g: (0, 0)),
        ],
        out_specs=[
            pl.BlockSpec((SEQ, GROUP), mine),
            pl.BlockSpec((SEQ, GROUP), mine),
            pl.BlockSpec((SEQ, GROUP), mine),
            pl.BlockSpec((SEQ, GROUP), mine),
            pl.BlockSpec((1, 1, 8, SEQ), lambda b, g: (b, g, 0, 0)),
            pl.BlockSpec((SEQ, D), token),
        ],
        out_shape=[
            jax.ShapeDtypeStruct((rows, D), LOW),
            jax.ShapeDtypeStruct((rows, D), LOW),
            jax.ShapeDtypeStruct((rows, D), LOW),
            jax.ShapeDtypeStruct((rows, D), LOW),
            jax.ShapeDtypeStruct((seqs, GROUPS, 8, SEQ), F32),
            jax.ShapeDtypeStruct((rows, D), F32),
        ],
        scratch_shapes=[pltpu.VMEM((SEQ, SEQ), F32)],
        compiler_params=pltpu.CompilerParams(vmem_limit_bytes=48 * MIB),
        cost_estimate=pl.CostEstimate(
            flops=rows * (8 * D * D + 4 * D * SEQ), bytes_accessed=20 * MIB, transcendentals=rows * SEQ * HEADS
        ),
        name="attention_forward",
    )(x, wq, wk, wv, bq, bv, seg.reshape(rows, 1), seg.reshape(seqs, 1, SEQ), wo, bo)


def attention_backward_kernel(
    x_ref, q_ref, k_ref, v_ref, ctx_ref, dctx_ref, lse_ref, seg_col_ref, seg_row_ref,
    wq_ref, wk_ref, wv_ref, dh1_ref,
    gwq_ref, gwk_ref, gwv_ref, gbq_ref, gbv_ref, dx_ref,
    xt_ref, acc_ref, ds_ref, dq_ref, dk_ref, dv_ref, wq_acc, wk_acc, wv_acc, mask_ref,
):
    group, row, seqs = pl.program_id(0), pl.program_id(1), pl.num_programs(1)

    @pl.when(group == 0)
    def _():
        xt_ref[row] = jnp.transpose(x_ref[...])
        acc_ref[row] = dh1_ref[...]
        mask_ref[row] = jnp.where(seg_col_ref[...] == seg_row_ref[0], 0.0, -1e30)

    head_of = lax.broadcasted_iota(jnp.int32, (8, GROUP), 1) // HEAD_DIM
    picks = (head_of == lax.broadcasted_iota(jnp.int32, (8, GROUP), 0)).astype(F32)
    product = ctx_ref[...].astype(F32) * dctx_ref[...].astype(F32)
    inner = lax.dot_general(
        picks, product, (((1,), (1,)), ((), ())),
        preferred_element_type=F32, precision=lax.Precision.HIGHEST,
    )
    lane = lax.broadcasted_iota(jnp.int32, (1, TILE), 1)
    scale = jnp.asarray(HEAD_DIM**-0.5, LOW)
    for pair in range(GROUP // TILE):
        lanes = slice(pair * TILE, (pair + 1) * TILE)
        dq_halves = []
        dk_halves = []
        dv_halves = []
        for half in range(2):
            mine = (lane // HEAD_DIM) == half
            head = 2 * pair + half
            dk_tiles = []
            dv_tiles = []
            for j in range(SEQ // KT):
                keys = slice(j * KT, (j + 1) * KT)
                span = near(j, KT)
                q_pair = q_ref[span, lanes] * scale
                dctx_pair = dctx_ref[span, lanes]
                scores = mm_t(jnp.where(mine, k_ref[keys, lanes], 0), q_pair)
                probs = jnp.exp(scores + mask_ref[row, keys, span] - lse_ref[0, 0, head : head + 1, span])
                d_probs = mm_t(jnp.where(mine, v_ref[keys, lanes], 0), dctx_pair)
                d_scores = (probs * (d_probs - inner[head : head + 1, span])).astype(LOW)
                ds_ref[keys, span] = d_scores
                dv_tiles.append(mm(probs.astype(LOW), dctx_pair))
                dk_tiles.append(mm(d_scores, q_pair))
            dk_halves.append(dk_tiles)
            dv_halves.append(dv_tiles)
            dq_tiles = []
            for i in range(SEQ // KT):
                span = near(i, KT)
                rows = slice(i * KT, (i + 1) * KT)
                dq_tiles.append(t_mm(ds_ref[span, rows], k_ref[span, lanes] * scale))
            dq_halves.append(dq_tiles)
        for i in range(SEQ // KT):
            rows = slice(i * KT, (i + 1) * KT)
            first = lane < HEAD_DIM
            dq_ref[rows, lanes] = jnp.where(first, dq_halves[0][i], dq_halves[1][i]).astype(LOW)
            dk_ref[rows, lanes] = jnp.where(first, dk_halves[0][i], dk_halves[1][i]).astype(LOW)
            dv_ref[rows, lanes] = jnp.where(first, dv_halves[0][i], dv_halves[1][i]).astype(LOW)
    dq, dk, dv = dq_ref[...], dk_ref[...], dv_ref[...]
    acc_ref[row] += mm_t(dq, wq_ref[...]) + mm_t(dk, wk_ref[...]) + mm_t(dv, wv_ref[...])
    xt = xt_ref[row]
    bias_q = jnp.sum(dq.astype(F32), axis=0, keepdims=True)
    bias_v = jnp.sum(dv.astype(F32), axis=0, keepdims=True)

    @pl.when(row == 0)
    def _():
        wq_acc[...] = mm(xt, dq)
        wk_acc[...] = mm(xt, dk)
        wv_acc[...] = mm(xt, dv)
        gbq_ref[...] = bias_q
        gbv_ref[...] = bias_v

    @pl.when(row > 0)
    def _():
        wq_acc[...] += mm(xt, dq)
        wk_acc[...] += mm(xt, dk)
        wv_acc[...] += mm(xt, dv)
        gbq_ref[...] += bias_q
        gbv_ref[...] += bias_v

    @pl.when(row == seqs - 1)
    def _():
        gwq_ref[...] = wq_acc[...].astype(LOW)
        gwk_ref[...] = wk_acc[...].astype(LOW)
        gwv_ref[...] = wv_acc[...].astype(LOW)

    dx_ref[...] = acc_ref[row].astype(LOW)


def attention_backward(x, seg, q, k, v, ctx, dctx, lse, wq, wk, wv, dh1):
    rows = x.shape[0]
    seqs = rows // SEQ
    token = lambda g, b: (b, 0)
    mine = lambda g, b: (b, g)
    column = lambda g, b: (0, g)
    return pl.pallas_call(
        attention_backward_kernel,
        grid=(GROUPS, seqs),
        in_specs=[pl.BlockSpec((SEQ, D), token)]
        + [pl.BlockSpec((SEQ, GROUP), mine)] * 5
        + [
            pl.BlockSpec((1, 1, 8, SEQ), lambda g, b: (b, g, 0, 0)),
            pl.BlockSpec((SEQ, 1), token),
            pl.BlockSpec((1, 1, SEQ), lambda g, b: (b, 0, 0)),
        ]
        + [pl.BlockSpec((D, GROUP), column)] * 3
        + [pl.BlockSpec((SEQ, D), token)],
        out_specs=[pl.BlockSpec((D, GROUP), column)] * 3
        + [pl.BlockSpec((1, GROUP), column)] * 2
        + [pl.BlockSpec((SEQ, D), token)],
        out_shape=[jax.ShapeDtypeStruct((D, D), LOW)] * 3
        + [jax.ShapeDtypeStruct((1, D), F32)] * 2
        + [jax.ShapeDtypeStruct((rows, D), LOW)],
        scratch_shapes=[
            pltpu.VMEM((seqs, D, SEQ), LOW),
            pltpu.VMEM((seqs, SEQ, D), F32),
            pltpu.VMEM((SEQ, SEQ), LOW),
            pltpu.VMEM((SEQ, GROUP), LOW),
            pltpu.VMEM((SEQ, GROUP), LOW),
            pltpu.VMEM((SEQ, GROUP), LOW),
            pltpu.VMEM((D, GROUP), F32),
            pltpu.VMEM((D, GROUP), F32),
            pltpu.VMEM((D, GROUP), F32),
            pltpu.VMEM((seqs, SEQ, SEQ), F32),
        ],
        compiler_params=pltpu.CompilerParams(vmem_limit_bytes=48 * MIB),
        cost_estimate=pl.CostEstimate(
            flops=rows * (12 * D * D + 10 * D * SEQ), bytes_accessed=30 * MIB, transcendentals=rows * SEQ * HEADS
        ),
        name="attention_backward",
    )(x, q, k, v, ctx, dctx, lse, seg.reshape(rows, 1), seg.reshape(seqs, 1, SEQ), wq, wk, wv, dh1)


FF = 3072
CHUNK = 768
ROWS = 256
EPS = 1e-05
ROOT = 0.7978845608028654
CUBE = 0.044715


def norm_parts(hidden):
    mean = jnp.mean(hidden, axis=1, keepdims=True)
    centred = hidden - mean
    inverse = lax.rsqrt(jnp.mean(centred * centred, axis=1, keepdims=True) + EPS)
    return centred * inverse, inverse


def norm_back(grad, gain, normed, inverse):
    scaled = grad * gain
    mean = jnp.mean(scaled, axis=1, keepdims=True)
    along = jnp.mean(scaled * normed, axis=1, keepdims=True)
    return inverse * (scaled - mean - normed * along)


def column_sum(array):
    return jnp.sum(array, axis=0, keepdims=True)


def gelu_and_slope(v):
    square = v * v
    bent = jnp.tanh(v * (ROOT + ROOT * CUBE * square))
    half = 0.5 + 0.5 * bent
    slope = half + (0.5 * v) * (1.0 - bent * bent) * (ROOT + 3.0 * ROOT * CUBE * square)
    return v * half, slope


def ffn_forward_kernel(
    h1_ref, cot_ref, wi_ref, wo_ref, bi_ref, bo_ref, g1_ref, s1_ref, g2_ref, s2_ref,
    out_ref, n1_ref, act_ref, slope_ref, db_ref, dh2_ref, gg2_ref, gs2_ref, gbo_ref,
    h2_ref,
):
    step = pl.program_id(0)
    tiles = [slice(i, i + ROWS) for i in range(0, h1_ref.shape[0], ROWS)]

    @pl.when(step == 0)
    def _():
        for rows in tiles:
            n, _ = norm_parts(h1_ref[rows, :])
            n1 = n * g1_ref[...] + s1_ref[...]
            n1_ref[rows, :] = n1.astype(LOW)
            h2_ref[rows, :] = n1 + bo_ref[...]

    for rows in tiles:
        pre = mm(n1_ref[rows, :], wi_ref[...]) + bi_ref[...]
        act, slope = gelu_and_slope(pre)
        act = act.astype(LOW)
        act_ref[rows, :] = act
        slope_ref[rows, :] = slope.astype(LOW)
        h2_ref[rows, :] += mm(act, wo_ref[...])

    @pl.when(step == pl.num_programs(0) - 1)
    def _():
        sums = [jnp.zeros((1, D), F32)] * 3
        for rows in tiles:
            n, inverse = norm_parts(h2_ref[rows, :])
            out_ref[rows, :] = (n * g2_ref[...] + s2_ref[...]).astype(LOW)
            cot = cot_ref[rows, :].astype(F32)
            dh2 = norm_back(cot, g2_ref[...], n, inverse)
            dh2_ref[rows, :] = dh2
            db = dh2.astype(LOW)
            db_ref[rows, :] = db
            new = (column_sum(cot * n), column_sum(cot), column_sum(db.astype(F32)))
            sums = [a + b for a, b in zip(sums, new)]
        gg2_ref[...], gs2_ref[...], gbo_ref[...] = sums


def ffn_forward(h1, cot, wi, wo, bi, bo, g1, s1, g2, s2):
    rows = h1.shape[0]
    all_rows = pl.BlockSpec((rows, D), lambda c: (0, 0))
    vector = pl.BlockSpec((1, D), lambda c: (0, 0))
    chunk = pl.BlockSpec((rows, CHUNK), lambda c: (0, c))
    return pl.pallas_call(
        ffn_forward_kernel,
        grid=(FF // CHUNK,),
        in_specs=[
            all_rows,
            all_rows,
            pl.BlockSpec((D, CHUNK), lambda c: (0, c)),
            pl.BlockSpec((CHUNK, D), lambda c: (c, 0)),
            pl.BlockSpec((1, CHUNK), lambda c: (0, c)),
            vector, vector, vector, vector, vector,
        ],
        out_specs=[all_rows, all_rows, chunk, chunk, all_rows, all_rows, vector, vector, vector],
        out_shape=[
            jax.ShapeDtypeStruct((rows, D), LOW),
            jax.ShapeDtypeStruct((rows, D), LOW),
            jax.ShapeDtypeStruct((rows, FF), LOW),
            jax.ShapeDtypeStruct((rows, FF), LOW),
            jax.ShapeDtypeStruct((rows, D), LOW),
            jax.ShapeDtypeStruct((rows, D), F32),
        ]
        + [jax.ShapeDtypeStruct((1, D), F32)] * 3,
        scratch_shapes=[pltpu.VMEM((rows, D), F32)],
        compiler_params=pltpu.CompilerParams(vmem_limit_bytes=56 * MIB),
        cost_estimate=pl.CostEstimate(flops=4 * rows * D * FF, bytes_accessed=34 * MIB, transcendentals=rows * FF),
        name="ffn_forward",
    )(h1, cot, wi, wo, bi, bo, g1, s1, g2, s2)


def ffn_backward_kernel(
    h1_ref, n1_ref, act_ref, slope_ref, db_ref, dh2_ref, ctx_ref, wi_ref, wo_ref, wout_ref, g1_ref,
    gwi_ref, gwo_ref, gbi_ref, gwout_ref, dctx_ref, dh1_ref, gg1_ref, gs1_ref, gbout_ref,
    n1t_ref, dn1_ref, dpre_ref, da_ref,
):
    step = pl.program_id(0)
    tiles = [slice(i, i + ROWS) for i in range(0, h1_ref.shape[0], ROWS)]

    @pl.when(step == 0)
    def _():
        n1t_ref[...] = jnp.transpose(n1_ref[...])
        dn1_ref[...] = dh2_ref[...]

    bias = jnp.zeros((1, CHUNK), F32)
    for rows in tiles:
        dpre = (mm_t(db_ref[rows, :], wo_ref[...]) * slope_ref[rows, :].astype(F32)).astype(LOW)
        dpre_ref[rows, :] = dpre
        bias += column_sum(dpre.astype(F32))
        dn1_ref[rows, :] += mm_t(dpre, wi_ref[...])
    gbi_ref[...] = bias
    gwo_ref[...] = t_mm(act_ref[...], db_ref[...]).astype(LOW)
    gwi_ref[...] = mm(n1t_ref[...], dpre_ref[...]).astype(LOW)

    @pl.when(step == pl.num_programs(0) - 1)
    def _():
        sums = [jnp.zeros((1, D), F32)] * 3
        for rows in tiles:
            n, inverse = norm_parts(h1_ref[rows, :])
            dn1 = dn1_ref[rows, :]
            dh1 = norm_back(dn1, g1_ref[...], n, inverse)
            dh1_ref[rows, :] = dh1
            da = dh1.astype(LOW)
            da_ref[rows, :] = da
            dctx_ref[rows, :] = mm_t(da, wout_ref[...]).astype(LOW)
            new = (column_sum(dn1 * n), column_sum(dn1), column_sum(da.astype(F32)))
            sums = [a + b for a, b in zip(sums, new)]
        gg1_ref[...], gs1_ref[...], gbout_ref[...] = sums
        gwout_ref[...] = t_mm(ctx_ref[...], da_ref[...]).astype(LOW)


def ffn_backward(h1, n1, act, slope, db, dh2, ctx, wi, wo, wout, g1):
    rows = h1.shape[0]
    all_rows = pl.BlockSpec((rows, D), lambda c: (0, 0))
    once = pl.BlockSpec((rows, D), lambda c: (0, 0), pipeline_mode=pl.Buffered(1))
    vector = pl.BlockSpec((1, D), lambda c: (0, 0))
    chunk = pl.BlockSpec((rows, CHUNK), lambda c: (0, c))
    inner = pl.BlockSpec((D, CHUNK), lambda c: (0, c))
    outer = pl.BlockSpec((CHUNK, D), lambda c: (c, 0))
    square = pl.BlockSpec((D, D), lambda c: (0, 0))
    return pl.pallas_call(
        ffn_backward_kernel,
        grid=(FF // CHUNK,),
        in_specs=[once, once, chunk, chunk, once, once, once, inner, outer, square, vector],
        out_specs=[inner, outer, pl.BlockSpec((1, CHUNK), lambda c: (0, c)), square, all_rows, all_rows]
        + [vector] * 3,
        out_shape=[
            jax.ShapeDtypeStruct((D, FF), LOW),
            jax.ShapeDtypeStruct((FF, D), LOW),
            jax.ShapeDtypeStruct((1, FF), F32),
            jax.ShapeDtypeStruct((D, D), LOW),
            jax.ShapeDtypeStruct((rows, D), LOW),
            jax.ShapeDtypeStruct((rows, D), F32),
        ]
        + [jax.ShapeDtypeStruct((1, D), F32)] * 3,
        scratch_shapes=[
            pltpu.VMEM((D, rows), LOW),
            pltpu.VMEM((rows, D), F32),
            pltpu.VMEM((rows, CHUNK), LOW),
            pltpu.VMEM((rows, D), LOW),
        ],
        compiler_params=pltpu.CompilerParams(vmem_limit_bytes=60 * MIB),
        cost_estimate=pl.CostEstimate(
            flops=8 * rows * D * FF + 4 * rows * D * D, bytes_accessed=46 * MIB, transcendentals=0
        ),
        name="ffn_backward",
    )(h1, n1, act, slope, db, dh2, ctx, wi, wo, wout, g1)


AXES = ("dp", "fsdp")
MATRICES = (0, 2, 3, 5, 9, 11)
VECTORS = (1, 4, 6, 7, 8, 10, 12, 13, 14)


def to_rows(array, lead):
    columns = array.shape[-1]
    if columns == D:
        return array
    return jnp.concatenate([array[..., i : i + D] for i in range(0, columns, D)], axis=lead)


def gather_params(params):
    pieces = [to_rows(params[i], 0) for i in MATRICES]
    vector = jnp.concatenate([params[i] for i in VECTORS])
    pieces.append(jnp.pad(vector, (0, -vector.size % D)).reshape(-1, D))
    packed = jnp.concatenate(pieces, axis=0)
    whole = lax.all_gather(packed, AXES, axis=0, tiled=False)
    count = whole.shape[0]
    full = [None] * len(params)
    start = 0
    for i in MATRICES:
        rows, columns = params[i].shape
        blocks = []
        for _ in range(columns // D):
            blocks.append(whole[:, start : start + rows].reshape(count * rows, D))
            start += rows
        full[i] = jnp.concatenate(blocks, axis=1)
    vectors = whole[:, start:].reshape(count, -1).astype(F32)
    start = 0
    for i in VECTORS:
        size = params[i].size
        full[i] = vectors[:, start : start + size].reshape(1, -1)
        start += size
    return tuple(full)


def scatter_grads(grads):
    count = lax.axis_size(AXES)
    low = [grad.astype(LOW) for grad in grads]
    pieces = [to_rows(low[i].reshape(count, -1, low[i].shape[1]), 1) for i in MATRICES]
    vector = jnp.concatenate([low[i].reshape(count, -1) for i in VECTORS], axis=1)
    vector = jnp.pad(vector, ((0, 0), (0, -vector.shape[1] % D)))
    pieces.append(vector.reshape(count, -1, D))
    packed = jnp.concatenate(pieces, axis=1)
    mine = lax.psum_scatter(packed, AXES, scatter_dimension=0, tiled=False)
    mine = mine.astype(F32)
    shards = [None] * len(grads)
    start = 0
    for i in MATRICES:
        rows, columns = grads[i].shape[0] // count, grads[i].shape[1]
        blocks = []
        for _ in range(columns // D):
            blocks.append(mine[start : start + rows])
            start += rows
        shards[i] = jnp.concatenate(blocks, axis=1)
    vectors = mine[start:].reshape(-1)
    start = 0
    for i in VECTORS:
        size = grads[i].size // count
        shards[i] = vectors[start : start + size]
        start += size
    return shards


def on_device(block_input, segment_ids, cotangent, *params):
    (
        w_query, b_query, w_key, w_value, b_value, w_out, b_out, gain_one, shift_one,
        w_inner, b_inner, w_outer, b_outer, gain_two, shift_two,
    ) = gather_params(params)
    x = block_input.reshape(-1, D)
    cot = cotangent.reshape(-1, D)
    q, k, v, ctx, lse, h1 = attention_forward(
        x, segment_ids, w_query, b_query, w_key, w_value, b_value, w_out, b_out
    )
    result, n1, act, slope, db, dh2, g_gain_two, g_shift_two, g_b_outer = ffn_forward(
        h1, cot, w_inner, w_outer, b_inner, b_outer, gain_one, shift_one, gain_two, shift_two
    )
    g_inner, g_outer, g_b_inner, g_out, dctx, dh1, g_gain_one, g_shift_one, g_b_out = ffn_backward(
        h1, n1, act, slope, db, dh2, ctx, w_inner, w_outer, w_out, gain_one
    )
    g_query, g_key, g_value, g_b_query, g_b_value, dx = attention_backward(
        x, segment_ids, q, k, v, ctx, dctx, lse, w_query, w_key, w_value, dh1
    )
    shards = scatter_grads(
        (g_query, g_b_query, g_key, g_value, g_b_value, g_out, g_b_out, g_gain_one, g_shift_one)
        + (g_inner, g_b_inner, g_outer, g_b_outer, g_gain_two, g_shift_two)
    )
    return (result.reshape(block_input.shape), dx.reshape(block_input.shape), *shards)


def solution(mesh):
    vector, matrix, rows = P(AXES), P(AXES, None), P(AXES, None, None)
    params = tuple(vector if i in VECTORS else matrix for i in range(15))
    return jax.shard_map(
        on_device,
        mesh=mesh,
        in_specs=(rows, matrix, rows) + params,
        out_specs=(rows, rows) + params,
        check_vma=False,
    )
```

time: 578 us -> 466 us (0.81); the launches traced: 569 us -> 465 us
  matrix products: 176 us -> 0 us
  Pallas kernels: 0 us -> 123 us
  other arithmetic: 45.7 us -> 8 us
  local copies, waits for them, and re-layouts: 73.6 us -> 50.4 us
  waiting for transfers between devices: 258 us -> 269 us
    dot_general x24 -> x0, matrix products: 176 us -> none  [the longest x6 33.6 us: matmul(): return jnp.dot(left, right, preferred_element_type=jnp.float32)]
    pallas_call x0 -> x4, Pallas kernels: none -> 123 us  [the longest x1 36.6 us: ffn_backward(): pl.pallas_call(ffn_backward_kernel, grid=(FF // CHUNK,), in_specs=[once,...]
    reduce_sum x9 -> x0, other arithmetic: 20.1 us -> none  [the longest x1 11.2 us: forward(): total = jnp.sum(jnp.exp(masked - row_max), axis=-1, keepdims=True)]
    convert_element_type x4 -> x8, other arithmetic: 22.9 us -> 4.54 us  [the longest x6 2.36 us: scatter_grads(): low = [grad.astype(LOW) for grad in grads]]
    convert_element_type x18 -> x0, local copies, waits for them, and re-layouts: 12.5 us -> none  [the longest x1 3.15 us: backward_attention(): d_values = jnp.einsum('bhqk,bqhd->bkhd', probs.astype(jnp.bfloat16), d_co...]
    reshape x4 -> x10, local copies, waits for them, and re-layouts: 13.5 us -> 4.98 us  [the longest x9 4.29 us: gather_params(): full[i] = vectors[:, start:start + size].reshape(1, -1)]
    reduce_scatter x1, waiting for transfers between devices: 155 us -> 163 us  [scatter_grads(): mine = lax.psum_scatter(packed, AXES, scatter_dimension=0, tiled=False)]
    unnamed x95 -> x49, local copies, waits for them, and re-layouts: 27 us -> 25.8 us
  transfers between devices with their start and end apart: 2 -> 2, of which waited for: 2 -> 2; matrix products, arithmetic and copies ran while one was open for 2% -> 0% of each run, Pallas kernels for 0% -> 0%
where the time goes in v2:
time: 466 us; the launch traced here: 465 us
  waiting for transfers between devices  269 us (58%)
  Pallas kernels  123 us (26%)
  local copies, waits for them, and re-layouts  50.4 us (11%)
  between operations  14.3 us (3%)
  other arithmetic  8 us (2%)
    reduce_scatter x1, waiting for transfers between devices, scatter_grads(): mine = lax.psum_scatter(packed, AXES, scatter_dimension=0, tiled=False)  163 us
    all_gather x1, waiting for transfers between devices, gather_params(): whole = lax.all_gather(packed, AXES, axis=0, tiled=False)  106 us
    pallas_call x1, Pallas kernels, ffn_backward(): pl.pallas_call(ffn_backward_kernel, grid=(FF // CHUNK,), in_specs=[once,...  36.6 us
    pallas_call x1, Pallas kernels, attention_backward(): pl.pallas_call(attention_backward_kernel, grid=(GROUPS, seqs), in_specs=[...  34.9 us
    pallas_call x1, Pallas kernels, ffn_forward(): pl.pallas_call(ffn_forward_kernel, grid=(FF // CHUNK,), in_specs=[all_row...  26 us
    unnamed x49, local copies, waits for them, and re-layouts  25.8 us
    pallas_call x1, Pallas kernels, attention_forward(): pl.pallas_call(attention_forward_kernel, grid=(seqs, GROUPS), in_specs=[p...  25.7 us
  transfers between devices with their start and end apart: 2, of which 2 were waited for; matrix products, arithmetic and copies ran while one was open for 0% of the time, Pallas kernels for 0%

profile of v2, /device:TPU:0, one launch (start us, length us, event | category | flops | bytes accessed | tf_op | source)
XLA Modules:
  0.0 465.4 jit_solution(7457131584468618730)
XLA Ops:
  13.4 0.9 constant_dynamic-update-slice_fusion.1
  14.3 6.1 %concatenate.18 = bf16[288]{0:T(512)(128)(2,1)S(1)} concatenate(bf16[24]{0:T(256)(128)(2,1)} %param.22, bf16[24]{0:T(256)(128)(2,1)} %param.25, bf16[24]{0:T(256)(128)(2,1)} %param.27, bf16[24]{0:T(256)(128)(2,1)} %param.28, bf16[24]{0:T(256)(128)(2,1)} %param.29, bf16[96]{0:T(256)(128)(2,1)} %param.31, bf16[24]{0:T(256)(128)(2,1)} %param.33, bf16[24]{0:T(256)(128)(2,1)} %param.34, ...), dimensions={0} | concatenate | bytes 1152 | tf_op jit(solution)/shard_map/concatenate | solution.py:465
  22.9 106.1 %all-gather.4.cloned.1.call-done = bf16[32,289,768]{2,1,0:T(8,128)(2,1)} async-done(((bf16[1,289,768]{2,1,0:T(8,128)(2,1)}), bf16[32,289,768]{2,1,0:T(8,128)(2,1)}) %all-gather.4.cloned.1.call-update) | async-done | bytes 14204944 | tf_op jit(solution)/shard_map/all_gather | solution.py:468
  129.0 1.0 slice_convert_fusion
  134.6 4.1 fusion
  138.7 2.7 pad_maximum_fusion.wi_ref
  142.0 25.7 %attention_forward.1 = (bf16[1024,768]{1,0:T(8,128)(2,1)}, bf16[1024,768]{1,0:T(8,128)(2,1)}, bf16[1024,768]{1,0:T(8,128)(2,1)}, bf16[1024,768]{1,0:T(8,128)(2,1...) custom-call(bf16[1024,768]{1,0:T(8,128)(2,1)} %bitcast.100, bf16[768,768]{1,0:T(8,128)(2,1)S(1)} %bitcast.71, ...), custom_call_target="tpu_custom_call" | custom-call | flops 6442450944 | bytes 20971520 | tf_op jit(solution)/shard_map/attention_forward/pallas_call | solution.py:92
  167.7 4.9 %slice.274 = bf16[32,96,768]{2,1,0:T(8,128)(2,1)} slice(bf16[32,289,768]{2,1,0:T(8,128)(2,1)} %all-gather.4.cloned.1.call-done), slice={[0:32], [192:288], [0:768]} | slice | bytes 9437184 | tf_op jit(solution)/shard_map/slice | solution.py:476
  172.6 26.0 %ffn_forward.1 = (bf16[1024,768]{1,0:T(8,128)(2,1)}, bf16[1024,768]{1,0:T(8,128)(2,1)}, bf16[1024,3072]{1,0:T(8,128)(2,1)}, bf16[1024,3072]{1,0:T(8,128)(2,1)}, ...) custom-call(f32[1024,768]{1,0:T(8,128)} %get-tuple-element.47.h1_ref, ...), custom_call_target="tpu_custom_call" | custom-call | flops 9663676416 | bytes 35651584 | tf_op jit(solution)/shard_map/ffn_forward/pallas_call | solution.py:345
  198.6 36.6 %ffn_backward.1 = (bf16[768,3072]{1,0:T(8,128)(2,1)}, bf16[3072,768]{1,0:T(8,128)(2,1)}, f32[1,3072]{1,0:T(1,128)}, bf16[768,768]{1,0:T(8,128)(2,1)}, bf16[1024,...) custom-call(f32[1024,768]{1,0:T(8,128)} %get-tuple-element.47.h1_ref, ...), custom_call_target="tpu_custom_call" | custom-call | flops 21743271936 | bytes 48234496 | tf_op jit(solution)/shard_map/ffn_backward/pallas_call | solution.py:422
  235.3 34.9 %attention_backward.1 = (bf16[768,768]{1,0:T(8,128)(2,1)S(1)}, bf16[768,768]{1,0:T(8,128)(2,1)S(1)}, bf16[768,768]{1,0:T(8,128)(2,1)S(1)}, f32[1,768]{1,0:T(1,12...) custom-call(bf16[1024,768]{1,0:T(8,128)(2,1)} %bitcast.101, bf16[1024,768]{1,0:T(8,128)(2,1)} %get-tuple-element.49.q_ref, ...), custom_call_target="tpu_custom_call" | custom-call | flops 11274289152 | bytes 31457280 | tf_op jit(solution)/shard_map/attention_backward/pallas_call | solution.py:228
  270.1 1.0 copy-done.3
  271.1 1.0 copy-done.4
  275.5 2.5 constant_dynamic-update-slice_fusion.14
  278.1 2.4 constant_dynamic-update-slice_fusion.13
  280.5 1.2 constant_dynamic-update-slice_fusion.12
  281.7 1.1 constant_dynamic-update-slice_fusion.11
  282.8 1.2 slice_dynamic-update-slice_fusion.3
  284.0 1.2 slice_dynamic-update-slice_fusion.2
  285.1 1.2 slice_dynamic-update-slice_fusion.1
  286.3 1.2 slice_dynamic-update-slice_fusion
  287.5 2.5 constant_dynamic-update-slice_fusion.10
  290.8 163.3 %reduce-scatter.2.cloned.1.call-done = bf16[1,289,768]{2,1,0:T(8,128)(2,1)} async-done(((bf16[32,289,768]{2,1,0:T(8,128)(2,1)}), bf16[1,289,768]{2,1,0:T(8,128)(2,1)}) %reduce-scatter.2.cloned.1.call-update) | async-done | bytes 443920 | tf_op jit(solution)/shard_map/reduce_scatter | solution.py:496
  454.0 1.1 convert_bitcast_fusion
  (79 shorter events, 21.2 us)
Async XLA Ops:
  7.2 121.8 %all-gather.4.cloned.1.call-start = ((), (), s32[]{:S(2)}) async-start(), calls=%async_computation.2 | async-start | bytes 15003648 | tf_op jit(solution)/shard_map/all_gather | solution.py:468
  20.5 0.8 copy-start.9
  21.2 432.8 %reduce-scatter.2.cloned.1.call-start = ((), (), s32[]{:S(2)}) async-start(), calls=%async_computation.1 | async-start | bytes 15003648 | tf_op jit(solution)/shard_map/reduce_scatter | solution.py:496
  138.7 2.8 copy-start
  138.7 2.9 copy-start.1
  138.7 3.3 copy-start.2
  167.7 4.9 %copy-start.5 = (f32[2,3,8,512]{3,2,1,0:T(8,128)}, f32[2,3,8,512]{3,2,1,0:T(8,128)S(1)}, u32[]{:S(2)}) copy-start(f32[2,3,8,512]{3,2,1,0:T(8,128)S(1)} %get-tuple-element.59.lse_ref) | copy-start | bytes 294916
  198.6 36.7 %copy-start.6 = (f32[2,3,8,512]{3,2,1,0:T(8,128)S(1)}, f32[2,3,8,512]{3,2,1,0:T(8,128)}, u32[]{:S(2)}) copy-start(f32[2,3,8,512]{3,2,1,0:T(8,128)} %copy-done.5) | copy-start | bytes 294916
  235.2 39.1 %copy-start.10 = (f32[1,3072]{1,0:T(1,128)S(1)}, f32[1,3072]{1,0:T(1,128)}, u32[]{:S(2)}) copy-start(f32[1,3072]{1,0:T(1,128)} %get-tuple-element.73) | copy-start | bytes 36868
  235.3 40.0 %copy-start.11 = (f32[1,768]{1,0:T(1,128)S(1)}, f32[1,768]{1,0:T(1,128)}, u32[]{:S(2)}) copy-start(f32[1,768]{1,0:T(1,128)} %get-tuple-element.74) | copy-start | bytes 9220
  270.1 1.0 copy-start.3
  271.1 1.0 copy-start.4
  272.2 9.5 %copy-start.8 = (bf16[768,768]{1,0:T(8,128)(2,1)S(1)}, bf16[768,768]{1,0:T(8,128)(2,1)}, u32[]{:S(2)}) copy-start(bf16[768,768]{1,0:T(8,128)(2,1)} %get-tuple-element.65) | copy-start | bytes 3538948
  275.5 7.3 %copy-start.7 = (bf16[768,3072]{1,0:T(8,128)(2,1)S(1)}, bf16[768,3072]{1,0:T(8,128)(2,1)}, u32[]{:S(2)}) copy-start(bf16[768,3072]{1,0:T(8,128)(2,1)} %get-tuple-element.66) | copy-start | bytes 14155780
  280.5 7.0 %slice-start = ((s8[4718592]{0:T(1024)(128)(4,1)}), s8[4194304]{0:T(1024)(128)(4,1)S(1)}, s32[]{:S(2)}) async-start(s8[4718592]{0:T(1024)(128)(4,1)} %bitcast.84), calls=%async_computation.3 | async-start | bytes 8388608
  282.8 4.7 %slice-start.1 = ((s8[4718592]{0:T(1024)(128)(4,1)}), s8[524288]{0:T(1024)(128)(4,1)S(1)}, s32[]{:S(2)}) async-start(s8[4718592]{0:T(1024)(128)(4,1)} %bitcast.84), calls=%async_computation.4 | async-start | bytes 1048576
Sparse Core Ops, SparseCore 0:
  21.4 107.6 all-gather.3
  290.9 163.0 reduce-scatter.1
